TPU v7x, 128 devices: a whole 4x4x4 slice. The times are simulated.
128 devices in a mesh: sub: 16 (over y, z), grp: 8 (over x, core).
Axes of the slice: x: 4, y: 4, z: 4, core: 2. Of those that a mesh axis runs over, the one named last changes fastest.
Arguments:
- interior_res: bfloat16 [1024, 32, 256], P(('sub', 'grp')), may hold values from -6 to 6
- interface_res: bfloat16 [1024, 32, 512], P(('sub', 'grp')), may hold values from -6 to 6
- interior_inv: bfloat16 [1024, 256, 256], P(('sub', 'grp')), may hold values from -0.375 to 0.375
- coupling: bfloat16 [1024, 512, 256], P(('sub', 'grp')), may hold values from -0.375 to 0.375
- schur_inv: bfloat16 [1024, 512, 512], P(('sub', 'grp')), may hold values from -0.25 to 0.25
- coarse_inv: bfloat16 [512, 128, 128], P('grp'), may hold values from -0.5 to 0.5
- coarse_part: int32 [524288, 1], P(('sub', 'grp')), may hold values from 0 to 127; in each aligned block of 4096 rows (0 to 4095, 4096 to 8191, ...) at most 64 rows name the same one
- coarse_slot: int32 [524288], P(('sub', 'grp')), may hold values from 0 to 511
- live_count: int32 [1024], P(('sub', 'grp')), may hold values from 128 to 512
Outputs:
- interior_update: bfloat16 [1024, 32, 256], P(('sub', 'grp'))
- interface_update: bfloat16 [1024, 32, 512], P(('sub', 'grp'))
Inputs may be any that keep to these rules, and one draw needn't show every extreme that they name: `coarse_part`: in each device's aligned block of 4096 rows no section is named by more than 64 rows, a bound that some block reaches.
All inputs are finite; a program needn't handle non-finite values.
Results may differ from a plain program's by a relative error of at most 0.0076.
Values may be sent and summed in bfloat16 or wider, within the bound.
No kernel may reach another device: no remote copies, remote signals or barrier semaphores. Data moves between devices by JAX's collectives and lax.ppermute only.
A program may use at most 64 MiB of HBM per device.

v0:
```python
import math

import jax
import jax.numpy as jnp
from jax import lax
from jax.sharding import PartitionSpec as P


def coarse_apply(right_side, inverse_blocks):
    vec_count = right_side.shape[0]
    block_size = inverse_blocks.shape[1]
    reshaped = right_side.reshape(vec_count, -1, block_size)
    solved = jnp.einsum(
        "kbj,bij->kbi", reshaped, inverse_blocks, preferred_element_type=jnp.float32
    )
    return solved.reshape(vec_count, -1).astype(jnp.bfloat16)


def spread_cols(values, target, total):
    width = math.gcd(total, 512)

    def spread_one_block(number):
        columns = number * width + lax.iota(jnp.int32, width)
        table = (target[:, None] == columns[None, :]).astype(jnp.bfloat16)
        return jnp.dot(values, table, preferred_element_type=jnp.float32)

    blocks = lax.map(spread_one_block, jnp.arange(total // width, dtype=jnp.int32))
    return jnp.transpose(blocks, (1, 0, 2)).reshape(values.shape[0], total)


def pick_cols(values, wanted):
    count = wanted.shape[0]
    width = math.gcd(count, 512)
    source = lax.iota(jnp.int32, values.shape[1])

    def pick_one_block(number):
        chosen = lax.dynamic_slice_in_dim(wanted, number * width, width, 0)
        table = (source[:, None] == chosen[None, :]).astype(jnp.bfloat16)
        return jnp.dot(values, table, preferred_element_type=jnp.float32)

    blocks = lax.map(pick_one_block, jnp.arange(count // width, dtype=jnp.int32))
    return jnp.transpose(blocks, (1, 0, 2)).reshape(values.shape[0], count).astype(jnp.bfloat16)


def place_in_section(section_list, sections):
    rows_dev = section_list.shape[0]
    width = math.gcd(rows_dev, 128)
    section_hot = (section_list[:, None] == jnp.arange(sections, dtype=jnp.int32)[None, :]).astype(
        jnp.float32
    )
    hot_blocks = section_hot.reshape(rows_dev // width, width, sections)
    lower = (
        lax.broadcasted_iota(jnp.int32, (width, width), 0)
        >= lax.broadcasted_iota(jnp.int32, (width, width), 1)
    ).astype(jnp.float32)
    within = jnp.einsum("ij,bjs->bis", lower, hot_blocks, precision=lax.Precision.HIGHEST)
    totals = within[:, -1, :]
    before = jnp.cumsum(totals, axis=0) - totals
    counted = (within + before[:, None, :]).reshape(rows_dev, sections)
    return jnp.sum((counted - 1.0) * section_hot, axis=1).astype(jnp.int32)


def with_slots(flattened, slot_values):
    upper = (slot_values // 256).astype(jnp.bfloat16)[None, :]
    lower = (slot_values % 256).astype(jnp.bfloat16)[None, :]
    return jnp.concatenate([flattened, upper, lower], axis=0)


def read_slots(received, vec_count):
    upper = received[vec_count].astype(jnp.int32)
    lower = received[vec_count + 1].astype(jnp.int32)
    return (received[:vec_count], upper * 256 + lower)


def on_device(
    interior_res,
    interface_res,
    interior_inv,
    coupling,
    schur_inv,
    coarse_inv,
    coarse_part,
    coarse_slot,
    live_count,
):
    sub_count, vec_count, interior = interior_res.shape
    boundary = interface_res.shape[2]
    owners = lax.axis_size("grp")
    subgroups = lax.axis_size("sub")
    sections = owners * subgroups
    rows_dev = sub_count * boundary
    capacity = 2 * rows_dev // sections
    piece_size = rows_dev // 8
    per_owner = coarse_inv.shape[0] * coarse_inv.shape[1]
    interior_pre = jnp.einsum(
        "sij,skj->ski", interior_inv, interior_res, preferred_element_type=jnp.float32
    ).astype(jnp.bfloat16)
    condensed = interface_res.astype(jnp.float32) - jnp.einsum(
        "sbi,ski->skb", coupling, interior_pre, preferred_element_type=jnp.float32
    )
    alive_mask = (
        lax.broadcasted_iota(jnp.int32, (sub_count, 1, boundary), 2) < live_count[:, None, None]
    )
    condensed = jnp.where(alive_mask, condensed, 0.0).astype(jnp.bfloat16)
    section_list = coarse_part[:, 0]
    owner_list = section_list % owners
    piece_list = section_list // owners
    position = place_in_section(section_list, sections)
    flattened = jnp.transpose(condensed, (1, 0, 2)).reshape(vec_count, rows_dev)
    destination = owner_list * (subgroups * capacity) + piece_list * capacity + position
    owner_slot = piece_list * piece_size + coarse_slot
    outgoing = spread_cols(
        with_slots(flattened, owner_slot), destination, sections * capacity
    ).astype(jnp.bfloat16)
    received = lax.all_to_all(outgoing, "grp", split_axis=1, concat_axis=1, tiled=True)
    recv_rows, recv_slots = read_slots(received, vec_count)
    partial_sum = spread_cols(recv_rows, recv_slots, per_owner)
    summed = lax.psum(partial_sum, "sub")
    coarse_sol = coarse_apply(summed.astype(jnp.bfloat16), coarse_inv)
    replies = pick_cols(coarse_sol, recv_slots)
    returned = lax.all_to_all(replies, "grp", split_axis=1, concat_axis=1, tiled=True)
    correction = pick_cols(returned, destination)
    correction = jnp.transpose(correction.reshape(vec_count, sub_count, boundary), (1, 0, 2))
    local_term = jnp.einsum(
        "sbc,skc->skb", schur_inv, condensed, preferred_element_type=jnp.float32
    )
    interface_update = jnp.where(
        alive_mask, local_term + correction.astype(jnp.float32), 0.0
    ).astype(jnp.bfloat16)
    extended = interior_res.astype(jnp.float32) - jnp.einsum(
        "sbi,skb->ski", coupling, interface_update, preferred_element_type=jnp.float32
    )
    interior_update = jnp.einsum(
        "sij,skj->ski",
        interior_inv,
        extended.astype(jnp.bfloat16),
        preferred_element_type=jnp.float32,
    ).astype(jnp.bfloat16)
    return (interior_update, interface_update)


def solution(mesh):
    in_specs = (
        P(("sub", "grp"), None, None),
        P(("sub", "grp"), None, None),
        P(("sub", "grp"), None, None),
        P(("sub", "grp"), None, None),
        P(("sub", "grp"), None, None),
        P("grp", None, None),
        P(("sub", "grp"), None),
        P(("sub", "grp")),
        P(("sub", "grp")),
    )
    out_specs = (P(("sub", "grp"), None, None), P(("sub", "grp"), None, None))
    return jax.shard_map(
        on_device, mesh=mesh, in_specs=in_specs, out_specs=out_specs, check_vma=False
    )
```

profile of v0, /device:TPU:1, one launch (start us, length us, event | category | flops | bytes accessed | tf_op | source)
XLA Modules:
  0.0 473.6 jit_solution(12313746118868401771)
XLA Ops:
  10.9 69.0 %while.46 = (s32[]{:T(128)}, bf16[16,34,512]{2,1,0:T(8,128)(2,1)}, s32[4096]{0:T(1024)}, s32[16]{0:T(128)S(1)}, bf16[34,4096]{1,0:T(8,128)(2,1)}, /*index=5*/s32[1]{0:T(128)}) while((s32[]{:T(128)}, bf16[16,34,512]{2,1,0:T(8,128)(2,1)}, s32[4096]{0:T(1024)}, s32[16]{0:T(128)S(1)}, bf16[34,4096]{1,0:T(8,128)(2,1)}, ...), condition=%wide.region_3.4_spmd.clone, body=%wide.region_2.3_spmd.sunk.clone | while | flops 144704000 | bytes 430689 | solution.py:27
  86.2 5.8 %all-to-all-start = ((bf16[34,8,1024]{2,0,1:T(8,128)(2,1)}), bf16[34,8,1024]{2,0,1:T(8,128)(2,1)}, u32[]{:S(2)}, u32[]{:S(2)}) async-start(bf16[34,8,1024]{2,0,1:T(8,128)(2,1)} %copy.27), calls=%async_computation | async-start | bytes 1310720 | tf_op jit(solution)/shard_map/all_to_all | solution.py:115
  92.8 10.0 %all-to-all-done = bf16[34,8,1024]{2,0,1:T(8,128)(2,1)} async-done(((bf16[34,8,1024]{2,0,1:T(8,128)(2,1)}), bf16[34,8,1024]{2,0,1:T(8,128)(2,1)}, u32[]{:S(2)}, u32[]{:S(2)}) %all-to-all-start) | async-done | bytes 557088 | tf_op jit(solution)/shard_map/all_to_all | solution.py:115
  106.5 88.7 %while.47 = (s32[]{:T(128)}, f32[16,32,512]{2,1,0:T(8,128)}, s32[8192]{0:T(1024)}, s32[16]{0:T(128)S(1)}, bf16[32,8192]{1,0:T(8,128)(2,1)}, /*index=5*/s32[1]{0:T(128)}) while((s32[]{:T(128)}, f32[16,32,512]{2,1,0:T(8,128)}, s32[8192]{0:T(1024)}, s32[16]{0:T(128)S(1)}, bf16[32,8192]{1,0:T(8,128)(2,1)}, /*index=5*/s32[1]{0:T(128)}) %tuple.96), condition=%wide.region_5.6_spmd.clone, body=%wide.region_4.5_spmd.sunk.clone | while | flops 272630272 | bytes 627297 | solution.py:27
  107.7 4.4 fusion.97
  113.2 4.4 fusion.97
  118.8 4.4 fusion.97
  124.3 4.4 fusion.97
  129.9 4.4 fusion.97
  135.4 4.4 fusion.97
  140.9 4.4 fusion.97
  146.5 4.4 fusion.97
  152.0 4.4 fusion.97
  157.6 4.4 fusion.97
  163.1 4.4 fusion.97
  168.7 4.4 fusion.97
  174.2 4.4 fusion.97
  179.8 4.4 fusion.97
  185.3 4.4 fusion.97
  190.9 4.4 fusion.97
  197.6 76.3 %all-reduce.1 = bf16[32,8192]{1,0:T(8,128)(2,1)} all-reduce(f32[32,8192]{1,0:T(8,128)} %bitcast.120), channel_id=1, replica_groups=mesh['sub'=16,'grp'=8] {'sub'}, use_global_device_ids=true, to_apply=%region_6.7 | all-reduce | flops 262144 | bytes 1572864 | tf_op jit(solution)/shard_map/psum | solution.py:118
  277.0 101.6 %while.48 = (s32[]{:T(128)}, bf16[16,32,512]{2,1,0:T(8,128)(2,1)}, s32[16]{0:T(128)S(1)}, s32[8192]{0:T(1024)}, bf16[32,8192]{1,0:T(8,128)(2,1)}, /*index=5*/s32[1]{0:T(128)}) while((s32[]{:T(128)}, bf16[16,32,512]{2,1,0:T(8,128)(2,1)}, s32[16]{0:T(128)S(1)}, s32[8192]{0:T(1024)}, bf16[32,8192]{1,0:T(8,128)(2,1)}, ...), condition=%wide.region_8.9_spmd.clone.clone, body=%wide.region_7.8_spmd.clone.sunk.clone | while | flops 272629760 | bytes 596611 | solution.py:41
  285.4 4.4 fusion.99
  291.7 4.4 fusion.99
  298.1 4.4 fusion.99
  304.4 4.4 fusion.99
  310.8 4.4 fusion.99
  317.1 4.4 fusion.99
  323.5 4.4 fusion.99
  329.8 4.4 fusion.99
  336.2 4.4 fusion.99
  342.5 4.4 fusion.99
  348.9 4.4 fusion.99
  355.2 4.4 fusion.99
  361.6 4.4 fusion.99
  367.9 4.4 fusion.99
  374.3 4.4 fusion.99
  384.9 19.1 %all-to-all-start.1 = ((bf16[32,8,1024]{2,0,1:T(8,128)(2,1)}), bf16[32,8,1024]{2,0,1:T(8,128)(2,1)}, u32[]{:S(2)}, u32[]{:S(2)}) async-start(bf16[32,8,1024]{2,0,1:T(8,128)(2,1)} %copy.33), calls=%async_computation.1 | async-start | bytes 1048576 | tf_op jit(solution)/shard_map/all_to_all | solution.py:121
  404.0 9.5 %all-to-all-done.1 = bf16[32,8,1024]{2,0,1:T(8,128)(2,1)} async-done(((bf16[32,8,1024]{2,0,1:T(8,128)(2,1)}), bf16[32,8,1024]{2,0,1:T(8,128)(2,1)}, u32[]{:S(2)}, u32[]{:S(2)}) %all-to-all-start.1) | async-done | bytes 524320 | tf_op jit(solution)/shard_map/all_to_all | solution.py:121
  415.3 50.9 %while.49 = (s32[]{:T(128)}, bf16[8,32,512]{2,1,0:T(8,128)(2,1)}, s32[8]{0:T(128)S(1)}, s32[4096]{0:T(1024)}, bf16[32,8192]{1,0:T(8,128)(2,1)}, /*index=5*/s32[1]{0:T(128)}) while((s32[]{:T(128)}, bf16[8,32,512]{2,1,0:T(8,128)(2,1)}, s32[8]{0:T(128)S(1)}, s32[4096]{0:T(1024)}, bf16[32,8192]{1,0:T(8,128)(2,1)}, ...), condition=%wide.region_10.11_spmd.clone.clone, body=%wide.region_9.10_spmd.clone.sunk.clone | while | flops 272629760 | bytes 596611 | solution.py:41
  417.3 4.4 fusion.101
  423.7 4.4 fusion.101
  430.0 4.4 fusion.101
  436.4 4.4 fusion.101
  442.8 4.4 fusion.101
  449.1 4.4 fusion.101
  455.5 4.4 fusion.101
  461.9 4.4 fusion.101
  (177 shorter events, 146.3 us)
Async XLA Ops:
  0.6 273.3 %copy-start = (bf16[64,128,128]{2,1,0:T(8,128)(2,1)S(1)}, bf16[64,128,128]{2,1,0:T(8,128)(2,1)}, u32[]{:S(2)}) copy-start(bf16[64,128,128]{2,1,0:T(8,128)(2,1)} %param.22) | copy-start | bytes 6291460
  0.6 1.8 copy-start.3
  0.7 3.1 copy-start.5
  0.7 4.4 copy-start.6
  0.7 5.0 %copy-start.1 = (bf16[8,256,256]{2,1,0:T(8,128)(2,1)S(1)}, bf16[8,256,256]{2,1,0:T(8,128)(2,1)}, u32[]{:S(2)}) copy-start(bf16[8,256,256]{2,1,0:T(8,128)(2,1)} %param.19) | copy-start | bytes 3145732
  0.7 5.0 %copy-start.2 = (bf16[8,32,256]{2,1,0:T(8,128)(2,1)S(1)}, bf16[8,32,256]{2,1,0:T(8,128)(2,1)}, u32[]{:S(2)}) copy-start(bf16[8,32,256]{2,1,0:T(8,128)(2,1)} %param.17) | copy-start | bytes 393220
  86.2 16.6 %all-to-all-start = ((bf16[34,8,1024]{2,0,1:T(8,128)(2,1)}), bf16[34,8,1024]{2,0,1:T(8,128)(2,1)}, u32[]{:S(2)}, u32[]{:S(2)}) async-start(bf16[34,8,1024]{2,0,1:T(8,128)(2,1)} %copy.27), calls=%async_computation | async-start | bytes 1310720 | tf_op jit(solution)/shard_map/all_to_all | solution.py:115
  384.9 28.5 %all-to-all-start.1 = ((bf16[32,8,1024]{2,0,1:T(8,128)(2,1)}), bf16[32,8,1024]{2,0,1:T(8,128)(2,1)}, u32[]{:S(2)}, u32[]{:S(2)}) async-start(bf16[32,8,1024]{2,0,1:T(8,128)(2,1)} %copy.33), calls=%async_computation.1 | async-start | bytes 1048576 | tf_op jit(solution)/shard_map/all_to_all | solution.py:121
  415.3 50.9 %copy-start.4 = (pred[8,512]{1,0:T(8,128)(4,1)S(1)}, pred[8,512]{1,0:T(8,128)(4,1)}, u32[]{:S(2)}) copy-start(pred[8,512]{1,0:T(8,128)(4,1)} %iota_compare_fusion.17) | copy-start | bytes 12292
where the time goes:
time: 477 us; the launch traced here: 474 us
  matrix products  238 us (50%)
  blocking collectives  76.3 us (16%)
  local copies, waits for them, and re-layouts  71.9 us (15%)
  loops' own time  35.1 us (7%)
  starting transfers between devices  24.8 us (5%)
  waiting for transfers between devices  19.5 us (4%)
  other arithmetic  7.01 us (1%)
    dot_general x32, matrix products, spread_one_block(): return jnp.dot(values, table, preferred_element_type=jnp.float32)  119 us
    dot_general x24, matrix products, pick_one_block(): return jnp.dot(values, table, preferred_element_type=jnp.float32)  105 us
    psum x1, blocking collectives, on_device(): summed = lax.psum(partial_sum, 'sub')  76.3 us
    dynamic_slice x48, local copies, waits for them, and re-layouts, spread_cols(): lax.map(spread_one_block, jnp.arange(total // width, dtype=jnp.int32))  28 us
    another operation x2, loops' own time, spread_cols(): lax.map(spread_one_block, jnp.arange(total // width, dtype=jnp.int32))  19.7 us
    all_to_all x1, starting transfers between devices, on_device(): lax.all_to_all(replies, 'grp', split_axis=1, concat_axis=1, tiled=True)  19.1 us
    dynamic_slice x24, local copies, waits for them, and re-layouts, pick_one_block(): chosen = lax.dynamic_slice_in_dim(wanted, number * width, width, 0)  18.2 us
    another operation x2, loops' own time, pick_cols(): lax.map(pick_one_block, jnp.arange(count // width, dtype=jnp.int32))  15.4 us
  transfers between devices with their start and end apart: 2, of which 2 were waited for; matrix products, arithmetic and copies ran while one was open for 0% of the time, Pallas kernels for 0%

commit v1 on v0

v1 whole, which is shorter than its diff:
```python
import jax
import jax.numpy as jnp
from jax import lax
from jax.experimental import pallas as pl
from jax.experimental.pallas import tpu as pltpu
from jax.sharding import PartitionSpec as P

F32 = jnp.float32
BF16 = jnp.bfloat16
AXES = ("sub", "grp")
CAP = 64
VMEM = pltpu.VMEM
HALF = 64


def dot_nn(left, right):
    return lax.dot_general(left, right, (((1,), (0,)), ((), ())), preferred_element_type=F32)


def dot_nt(left, right):
    return lax.dot_general(left, right, (((1,), (1,)), ((), ())), preferred_element_type=F32)


def low_half(rows):
    return lax.broadcasted_iota(jnp.int32, (rows, 128), 1) < HALF


def swap_pair(first, second):
    mask = low_half(first.shape[0])
    even = jnp.where(mask, first, pltpu.roll(second, HALF, 1))
    odd = jnp.where(mask, pltpu.roll(first, HALF, 1), second)
    return even, odd


def one_hot(count, index):
    rows = lax.broadcasted_iota(jnp.int32, (count, index.shape[1]), 0).astype(BF16)
    return jnp.where(rows == index.astype(BF16), 1.0, 0.0).astype(BF16)


def front_kernel(
    live_ref, part_ref, slot_ref, ires_ref, fres_ref, inv_hbm, cpl_hbm,
    cond_ref, out_ref, dest_ref,
    inv_ref, cpl_ref, lhs_ref, acc_ref, sem,
):
    subs, vecs, inner = ires_ref.shape
    face = fres_ref.shape[2]
    loads = []
    for s in range(subs):
        one = pltpu.make_async_copy(inv_hbm.at[s], inv_ref.at[s], sem.at[0, s])
        two = pltpu.make_async_copy(cpl_hbm.at[s], cpl_ref.at[s], sem.at[1, s])
        one.start()
        two.start()
        loads.append((one, two))

    width = 256
    sections = out_ref.shape[0]
    upper = (
        lax.broadcasted_iota(jnp.int32, (width, width), 0)
        <= lax.broadcasted_iota(jnp.int32, (width, width), 1)
    ).astype(F32).astype(BF16)
    ones = jnp.ones((width, width), BF16)
    section_row = lax.broadcasted_iota(jnp.int32, (sections, width), 0)
    before = jnp.zeros((sections, width), F32)
    for c in range(subs * face // width):
        cols = pl.ds(c * width, width)
        section = part_ref[:, cols]
        hot = section_row == section
        hot16 = jnp.where(hot, 1.0, 0.0).astype(BF16)
        counted = dot_nn(hot16, upper) + before
        place = jnp.sum(jnp.where(hot, counted, 0.0), axis=0, keepdims=True) - 1.0
        before = before + dot_nn(hot16, ones)
        dest_ref[:, cols] = section * CAP + place.astype(jnp.int32)

    groups = sections // 4
    group_row = lax.broadcasted_iota(jnp.int32, (groups, face), 0)
    for s in range(subs):
        loads[s][0].wait()
        loads[s][1].wait()
        pre = dot_nt(ires_ref[s], inv_ref[s]).astype(BF16)
        cond = fres_ref[s].astype(F32) - dot_nt(pre, cpl_ref[s])
        alive = lax.broadcasted_iota(jnp.int32, (vecs, face), 1) < live_ref[s]
        cond = jnp.where(alive, cond, 0.0).astype(BF16)
        cond_ref[s] = cond
        cols = pl.ds(s * face, face)
        dest = dest_ref[:, cols]
        group = lax.shift_right_logical(dest, 8)
        hot = one_hot(256, jnp.bitwise_and(dest, 255))
        group16 = jnp.broadcast_to(group.astype(BF16), (vecs, face))
        for a in range(groups):
            lhs_ref[pl.ds(a * vecs, vecs), :] = jnp.where(group16 == a, cond, jnp.zeros_like(cond))
        slot = slot_ref[:, cols]
        mine = group_row == group
        high = jnp.where(mine, lax.shift_right_logical(slot, 8).astype(F32), 0.0).astype(BF16)
        low = jnp.where(mine, jnp.bitwise_and(slot, 255).astype(F32), 0.0).astype(BF16)
        lhs_ref[pl.ds(groups * vecs, groups), :] = high
        lhs_ref[pl.ds(groups * vecs + groups, groups), :] = low
        part = dot_nt(lhs_ref[...], hot)
        if s == 0:
            acc_ref[...] = part
        else:
            acc_ref[...] += part

    kh = vecs // 2
    base = groups * vecs
    for a in range(groups):
        for h in range(2):
            lanes = pl.ds(h * 128, 128)
            first = acc_ref[pl.ds(a * vecs, kh), lanes]
            second = acc_ref[pl.ds(a * vecs + kh, kh), lanes]
            even, odd = swap_pair(first, second)
            slot_even, slot_odd = swap_pair(
                jnp.broadcast_to(acc_ref[pl.ds(base + a, 1), lanes], (8, 128)),
                jnp.broadcast_to(acc_ref[pl.ds(base + groups + a, 1), lanes], (8, 128)),
            )
            p = 4 * a + 2 * h
            out_ref[p, 0:kh, :] = even.astype(BF16)
            out_ref[p, kh:kh + 8, :] = slot_even.astype(BF16)
            out_ref[p + 1, 0:kh, :] = odd.astype(BF16)
            out_ref[p + 1, kh:kh + 8, :] = slot_odd.astype(BF16)


def local_kernel(schur_ref, cond_ref, out_ref):
    out_ref[0] = dot_nt(cond_ref[0], schur_ref[0])


def middle_kernel(recv_ref, inv_ref, out_ref, lhs_ref, hot_ref, high_ref):
    senders = recv_ref.shape[0]
    kh = out_ref.shape[1]
    vecs = 2 * kh
    for j in range(senders // 2):
        cols = pl.ds(j * 128, 128)
        first = recv_ref[2 * j].astype(F32)
        second = recv_ref[2 * j + 1].astype(F32)
        even, odd = swap_pair(first, second)
        high = even[kh:kh + 1]
        hot_ref[:, cols] = one_hot(256, odd[kh:kh + 1])
        high_ref[:, cols] = jnp.broadcast_to(high, (8, 128))
        data = jnp.concatenate([even[:kh], odd[:kh]], axis=0)
        top = jnp.broadcast_to(high, (vecs, 128)) > 0.5
        lhs_ref[0:vecs, cols] = jnp.where(top, 0.0, data).astype(BF16)
        lhs_ref[vecs:2 * vecs, cols] = jnp.where(top, data, 0.0).astype(BF16)
    summed = dot_nt(lhs_ref[...], hot_ref[...]).astype(BF16)
    halves = []
    for h in range(2):
        blocks = []
        for c in range(2):
            rhs = summed[h * vecs:(h + 1) * vecs, c * 128:(c + 1) * 128]
            blocks.append(dot_nt(rhs, inv_ref[2 * h + c]))
        halves.append(jnp.concatenate(blocks, axis=1))
    solved = jnp.concatenate(halves, axis=0).astype(BF16)
    chunk = 1024
    for c in range(senders * 64 // chunk):
        found = dot_nn(solved, hot_ref[:, pl.ds(c * chunk, chunk)])
        for i in range(chunk // 128):
            lanes = slice(i * 128, (i + 1) * 128)
            j = c * (chunk // 128) + i
            top = jnp.broadcast_to(high_ref[0:1, pl.ds(j * 128, 128)], (vecs, 128)) > 0.5
            reply = jnp.where(top, found[vecs:, lanes], found[:vecs, lanes])
            even, odd = swap_pair(reply[:kh], reply[kh:])
            out_ref[2 * j] = even.astype(BF16)
            out_ref[2 * j + 1] = odd.astype(BF16)


def back_kernel(
    live_ref, ret_ref, dest_ref, local_ref, ires_ref, inv_hbm, cpl_hbm,
    inner_ref, face_ref,
    inv_ref, cpl_ref, lhs_ref, sem,
):
    subs, vecs, inner = ires_ref.shape
    face = face_ref.shape[2]
    kh = vecs // 2
    loads = []
    for s in range(subs):
        one = pltpu.make_async_copy(inv_hbm.at[s], inv_ref.at[s], sem.at[0, s])
        two = pltpu.make_async_copy(cpl_hbm.at[s], cpl_ref.at[s], sem.at[1, s])
        one.start()
        two.start()
        loads.append((one, two))
    senders = ret_ref.shape[0]
    wide = lhs_ref.shape[1]
    groups = lhs_ref.shape[0] // vecs
    pairs = wide // 128
    for j in range(senders // 2):
        first = ret_ref[2 * j].astype(F32)
        second = ret_ref[2 * j + 1].astype(F32)
        even, odd = swap_pair(first, second)
        a, i = j // pairs, j % pairs
        lhs_ref[a * vecs:a * vecs + kh, i * 128:(i + 1) * 128] = even.astype(BF16)
        lhs_ref[a * vecs + kh:(a + 1) * vecs, i * 128:(i + 1) * 128] = odd.astype(BF16)
    shift = wide.bit_length() - 1
    for s in range(subs):
        dest = dest_ref[:, pl.ds(s * face, face)]
        group = lax.shift_right_logical(dest, shift)
        within = jnp.bitwise_and(dest, wide - 1)
        hot = jnp.concatenate([one_hot(256, within - 256 * g) for g in range(wide // 256)], axis=0)
        found = dot_nn(lhs_ref[...], hot)
        group_all = jnp.broadcast_to(group, (vecs, face))
        correction = jnp.zeros((vecs, face), F32)
        for a in range(groups):
            correction = jnp.where(group_all == a, found[a * vecs:(a + 1) * vecs], correction)
        alive = lax.broadcasted_iota(jnp.int32, (vecs, face), 1) < live_ref[s]
        update = jnp.where(alive, local_ref[s] + correction, 0.0).astype(BF16)
        face_ref[s] = update
        loads[s][0].wait()
        loads[s][1].wait()
        extended = (ires_ref[s].astype(F32) - dot_nn(update, cpl_ref[s])).astype(BF16)
        inner_ref[s] = dot_nt(extended, inv_ref[s]).astype(BF16)


def vmem(count):
    return [pl.BlockSpec(memory_space=VMEM)] * count


ANY = pl.BlockSpec(memory_space=pl.ANY)
SMEM = pl.BlockSpec(memory_space=pltpu.SMEM)


def on_device(
    interior_res,
    interface_res,
    interior_inv,
    coupling,
    schur_inv,
    coarse_inv,
    coarse_part,
    coarse_slot,
    live_count,
):
    subs, vecs, inner = interior_res.shape
    face = interface_res.shape[2]
    rows = subs * face
    sections = lax.axis_size("sub") * lax.axis_size("grp")
    kh = vecs // 2
    groups = sections // 4
    shape = jax.ShapeDtypeStruct

    condensed, outgoing, dest = pl.pallas_call(
        front_kernel,
        name="front",
        out_shape=(
            shape((subs, vecs, face), BF16),
            shape((sections, kh + 8, 128), BF16),
            shape((1, rows), jnp.int32),
        ),
        in_specs=[SMEM] + vmem(4) + [ANY, ANY],
        out_specs=tuple(vmem(3)),
        scratch_shapes=[
            VMEM((subs, inner, inner), BF16),
            VMEM((subs, face, inner), BF16),
            VMEM((groups * (vecs + 2), face), BF16),
            VMEM((groups * (vecs + 2), 256), F32),
            pltpu.SemaphoreType.DMA((2, subs)),
        ],
        cost_estimate=pl.CostEstimate(flops=3 * 10**9, bytes_accessed=5 * 10**6, transcendentals=0),
    )(
        live_count, coarse_part.reshape(1, rows), coarse_slot.reshape(1, rows),
        interior_res, interface_res, interior_inv, coupling,
    )

    received = lax.all_to_all(outgoing, AXES, split_axis=0, concat_axis=0, tiled=True)

    local = pl.pallas_call(
        local_kernel,
        name="local",
        grid=(subs,),
        out_shape=shape((subs, vecs, face), F32),
        in_specs=[
            pl.BlockSpec((1, face, face), lambda s: (s, 0, 0)),
            pl.BlockSpec((1, vecs, face), lambda s: (s, 0, 0)),
        ],
        out_specs=pl.BlockSpec((1, vecs, face), lambda s: (s, 0, 0)),
        cost_estimate=pl.CostEstimate(
            flops=2 * rows * vecs * face, bytes_accessed=5 * 10**6, transcendentals=0
        ),
    )(schur_inv, condensed)

    blocks = coarse_inv.shape[0] // lax.axis_size("sub")
    mine = lax.dynamic_slice_in_dim(coarse_inv, lax.axis_index("sub") * blocks, blocks, 0)
    replies = pl.pallas_call(
        middle_kernel,
        name="middle",
        out_shape=shape((sections, kh, 128), BF16),
        in_specs=vmem(2),
        out_specs=vmem(1)[0],
        scratch_shapes=[
            VMEM((2 * vecs, sections * CAP), BF16),
            VMEM((256, sections * CAP), BF16),
            VMEM((8, sections * CAP), F32),
        ],
        cost_estimate=pl.CostEstimate(flops=10**9, bytes_accessed=2 * 10**6, transcendentals=0),
    )(received, mine)

    returned = lax.all_to_all(replies, AXES, split_axis=0, concat_axis=0, tiled=True)

    return pl.pallas_call(
        back_kernel,
        name="back",
        out_shape=(shape((subs, vecs, inner), BF16), shape((subs, vecs, face), BF16)),
        in_specs=[SMEM] + vmem(4) + [ANY, ANY],
        out_specs=tuple(vmem(2)),
        scratch_shapes=[
            VMEM((subs, inner, inner), BF16),
            VMEM((subs, face, inner), BF16),
            VMEM((8 * vecs, sections * CAP // 8), BF16),
            pltpu.SemaphoreType.DMA((2, subs)),
        ],
        cost_estimate=pl.CostEstimate(flops=3 * 10**9, bytes_accessed=6 * 10**6, transcendentals=0),
    )(live_count, returned, dest, local, interior_res, interior_inv, coupling)


def solution(mesh):
    rows = P(AXES)
    in_specs = (rows, rows, rows, rows, rows, P("grp"), rows, rows, rows)
    return jax.shard_map(
        on_device, mesh=mesh, in_specs=in_specs, out_specs=(rows, rows), check_vma=False
    )
```

time: 477 us -> 75.7 us (0.16)
  matrix products: 238 us -> 0 us
  blocking collectives: 76.3 us -> 0 us
  local copies, waits for them, and re-layouts: 71.9 us -> 2.35 us
  loops' own time: 35.1 us -> 0 us
  Pallas kernels: 0 us -> 33.4 us
  starting transfers between devices: 24.8 us -> 16 us
  other arithmetic: 7.01 us -> 0 us
    dot_general x61 -> x0, matrix products: 238 us -> none  [the longest x32 119 us: spread_one_block(): return jnp.dot(values, table, preferred_element_type=jnp.float32)]
    psum x1 -> x0, blocking collectives: 76.3 us -> none  [on_device(): summed = lax.psum(partial_sum, 'sub')]
    dynamic_slice x80 -> x1, local copies, waits for them, and re-layouts: 50.9 us -> 0.67 us  [on_device(): lax.dynamic_slice_in_dim(coarse_inv, lax.axis_index('sub') * blocks, bloc...]
    another operation x4 -> x0, loops' own time: 35.1 us -> none  [the longest x2 19.7 us: spread_cols(): lax.map(spread_one_block, jnp.arange(total // width, dtype=jnp.int32))]
    pallas_call x0 -> x4, Pallas kernels: none -> 33.4 us  [the longest x1 11.2 us: on_device(): pl.pallas_call(front_kernel, name='front', out_shape=(shape((subs, vecs,...]
    convert_element_type x7 -> x0, local copies, waits for them, and re-layouts: 13.5 us -> none  [the longest x3 6.32 us: on_device(): outgoing = spread_cols(with_slots(flattened, owner_slot), destination, se...]
    all_to_all x2, starting transfers between devices: 24.8 us -> 16 us  [the longest x1 11.5 us: on_device(): lax.all_to_all(outgoing, AXES, split_axis=0, concat_axis=0, tiled=True)]
  transfers between devices with their start and end apart: 2 -> 2, of which waited for: 2 -> 2; matrix products, arithmetic and copies ran while one was open for 0% -> 1% of each run, Pallas kernels for 0% -> 9%
where the time goes in v1:
time: 75.7 us; the launch traced here: 75.2 us
  Pallas kernels  33.4 us (44%)
  waiting for transfers between devices  22.7 us (30%)
  starting transfers between devices  16 us (21%)
  local copies, waits for them, and re-layouts  2.35 us (3%)
  between operations  0.84 us (1%)
    all_to_all x1, waiting for transfers between devices, on_device(): lax.all_to_all(outgoing, AXES, split_axis=0, concat_axis=0, tiled=True)  15.7 us
    all_to_all x1, starting transfers between devices, on_device(): lax.all_to_all(outgoing, AXES, split_axis=0, concat_axis=0, tiled=True)  11.5 us
    pallas_call x1, Pallas kernels, on_device(): pl.pallas_call(front_kernel, name='front', out_shape=(shape((subs, vecs,...  11.2 us
    pallas_call x1, Pallas kernels, on_device(): pl.pallas_call(back_kernel, name='back', out_shape=(shape((subs, vecs, in...  8.2 us
    pallas_call x1, Pallas kernels, on_device(): pl.pallas_call(middle_kernel, name='middle', out_shape=shape((sections, k...  7.26 us
    all_to_all x1, waiting for transfers between devices, on_device(): lax.all_to_all(replies, AXES, split_axis=0, concat_axis=0, tiled=True)  6.95 us
    pallas_call x1, Pallas kernels, on_device(): pl.pallas_call(local_kernel, name='local', grid=(subs,), out_shape=shape(...  6.65 us
    all_to_all x1, starting transfers between devices, on_device(): lax.all_to_all(replies, AXES, split_axis=0, concat_axis=0, tiled=True)  4.52 us
  transfers between devices with their start and end apart: 2, of which 2 were waited for; matrix products, arithmetic and copies ran while one was open for 1% of the time, Pallas kernels for 9%

profile of v1, /device:TPU:1, one launch (start us, length us, event | category | flops | bytes accessed | tf_op | source)
XLA Modules:
  0.0 75.2 jit_solution(10846458386589388455)
XLA Ops:
  0.6 0.0 copy-start
  0.6 11.2 %front.1 = (bf16[8,32,512]{2,1,0:T(8,128)(2,1)}, bf16[128,24,128]{2,1,0:T(8,128)(2,1)}, s32[1,4096]{1,0:T(1,128)}) custom-call(s32[8]{0:T(128)} %live_ref.3, s32[1,4096]{1,0:T(1,128)} %bitcast.2, s32[1,4096]{1,0:T(1,128)} %bitcast.3, bf16[8,32,256]{2,1,0:T(8,128)(2,1)} %ires_ref.3, bf16[8,32,512]{2,1,0:T(8,128)(2,1)} %fres_ref.1, ...), custom_call_target="tpu_custom_call" | custom-call | flops 3000000000 | bytes 5000000 | tf_op jit(solution)/shard_map/front/pallas_call | solution.py:237
  11.9 11.5 %all-to-all-start = ((bf16[128,24,128]{2,1,0:T(8,128)(2,1)}), bf16[128,24,128]{2,1,0:T(8,128)(2,1)S(1)}, u32[]{:S(2)}, u32[]{:S(2)}) async-start(bf16[128,24,128]{2,1,0:T(8,128)(2,1)} %get-tuple-element.5), calls=%async_computation | async-start | bytes 1572864 | tf_op jit(solution)/shard_map/all_to_all | solution.py:260
  23.4 0.0 copy-done
  23.4 0.7 constant_dynamic-slice_fusion.inv_ref
  24.1 15.7 %all-to-all-done.recv_ref = bf16[128,24,128]{2,1,0:T(8,128)(2,1)S(1)} async-done(((bf16[128,24,128]{2,1,0:T(8,128)(2,1)}), bf16[128,24,128]{2,1,0:T(8,128)(2,1)S(1)}, u32[]{:S(2)}, u32[]{:S(2)}) %all-to-all-start) | async-done | bytes 786464 | tf_op jit(solution)/shard_map/all_to_all | solution.py:260
  39.8 0.0 copy-start.1
  39.8 0.9 %copy-done.1 = bf16[128,24,128]{2,1,0:T(8,128)(2,1)} copy-done((bf16[128,24,128]{2,1,0:T(8,128)(2,1)}, bf16[128,24,128]{2,1,0:T(8,128)(2,1)S(1)}, u32[]{:S(2)}) %copy-start.1) | copy-done | bytes 786456
  40.7 7.3 %middle.1 = bf16[128,16,128]{2,1,0:T(8,128)(2,1)} custom-call(bf16[128,24,128]{2,1,0:T(8,128)(2,1)} %copy-done.1, bf16[4,128,128]{2,1,0:T(8,128)(2,1)} %constant_dynamic-slice_fusion.inv_ref), custom_call_target="tpu_custom_call" | custom-call | flops 1000000000 | bytes 2000000 | tf_op jit(solution)/shard_map/middle/pallas_call | solution.py:279
  47.9 4.5 %all-to-all-start.1 = ((bf16[128,16,128]{2,1,0:T(8,128)(2,1)}), bf16[128,16,128]{2,1,0:T(8,128)(2,1)S(1)}, u32[]{:S(2)}, u32[]{:S(2)}) async-start(bf16[128,16,128]{2,1,0:T(8,128)(2,1)} %middle.1), calls=%async_computation.1 | async-start | bytes 1048576 | tf_op jit(solution)/shard_map/all_to_all | solution.py:293
  52.5 6.7 %local.1.local_ref = f32[8,32,512]{2,1,0:T(8,128)} custom-call(bf16[8,512,512]{2,1,0:T(8,128)(2,1)} %schur_ref.1, bf16[8,32,512]{2,1,0:T(8,128)(2,1)} %get-tuple-element.7.cond_ref), custom_call_target="tpu_custom_call" | custom-call | flops 134217728 | bytes 5000000 | tf_op jit(solution)/shard_map/local/pallas_call | solution.py:262
  59.1 7.0 %all-to-all-done.1.ret_ref = bf16[128,16,128]{2,1,0:T(8,128)(2,1)S(1)} async-done(((bf16[128,16,128]{2,1,0:T(8,128)(2,1)}), bf16[128,16,128]{2,1,0:T(8,128)(2,1)S(1)}, u32[]{:S(2)}, u32[]{:S(2)}) %all-to-all-start.1) | async-done | bytes 524320 | tf_op jit(solution)/shard_map/all_to_all | solution.py:293
  66.1 0.0 copy-start.2
  66.1 0.8 %copy-done.2 = bf16[128,16,128]{2,1,0:T(8,128)(2,1)} copy-done((bf16[128,16,128]{2,1,0:T(8,128)(2,1)}, bf16[128,16,128]{2,1,0:T(8,128)(2,1)S(1)}, u32[]{:S(2)}) %copy-start.2) | copy-done | bytes 524312
  66.9 8.2 %back.1 = (bf16[8,32,256]{2,1,0:T(8,128)(2,1)}, bf16[8,32,512]{2,1,0:T(8,128)(2,1)}) custom-call(s32[8]{0:T(128)} %live_ref.3, bf16[128,16,128]{2,1,0:T(8,128)(2,1)} %copy-done.2, s32[1,4096]{1,0:T(1,128)} %get-tuple-element.6.dest_ref, f32[8,32,512]{2,1,0:T(8,128)} %local.1.local_ref, bf16[8,32,256]{2,1,0:T(8,128)(2,1)} %ires_ref.3, ...), custom_call_target="tpu_custom_call" | custom-call | flops 3000000000 | bytes 6000000 | tf_op jit(solution)/shard_map/back/pallas_call | solution.py:295
Async XLA Ops:
  0.6 22.8 %copy-start = (bf16[64,128,128]{2,1,0:T(8,128)(2,1)S(1)}, bf16[64,128,128]{2,1,0:T(8,128)(2,1)}, u32[]{:S(2)}) copy-start(bf16[64,128,128]{2,1,0:T(8,128)(2,1)} %param.14) | copy-start | bytes 6291460
  11.9 27.9 %all-to-all-start = ((bf16[128,24,128]{2,1,0:T(8,128)(2,1)}), bf16[128,24,128]{2,1,0:T(8,128)(2,1)S(1)}, u32[]{:S(2)}, u32[]{:S(2)}) async-start(bf16[128,24,128]{2,1,0:T(8,128)(2,1)} %get-tuple-element.5), calls=%async_computation | async-start | bytes 1572864 | tf_op jit(solution)/shard_map/all_to_all | solution.py:260
  39.8 0.9 %copy-start.1 = (bf16[128,24,128]{2,1,0:T(8,128)(2,1)}, bf16[128,24,128]{2,1,0:T(8,128)(2,1)S(1)}, u32[]{:S(2)}) copy-start(bf16[128,24,128]{2,1,0:T(8,128)(2,1)S(1)} %all-to-all-done.recv_ref) | copy-start | bytes 2359300
  47.9 18.1 %all-to-all-start.1 = ((bf16[128,16,128]{2,1,0:T(8,128)(2,1)}), bf16[128,16,128]{2,1,0:T(8,128)(2,1)S(1)}, u32[]{:S(2)}, u32[]{:S(2)}) async-start(bf16[128,16,128]{2,1,0:T(8,128)(2,1)} %middle.1), calls=%async_computation.1 | async-start | bytes 1048576 | tf_op jit(solution)/shard_map/all_to_all | solution.py:293
  66.1 0.8 %copy-start.2 = (bf16[128,16,128]{2,1,0:T(8,128)(2,1)}, bf16[128,16,128]{2,1,0:T(8,128)(2,1)S(1)}, u32[]{:S(2)}) copy-start(bf16[128,16,128]{2,1,0:T(8,128)(2,1)S(1)} %all-to-all-done.1.ret_ref) | copy-start | bytes 1572868

commit v2 on v1

v2 whole, which is shorter than its diff:
```python
import jax
import jax.numpy as jnp
from jax import lax
from jax.experimental import pallas as pl
from jax.experimental.pallas import tpu as pltpu
from jax.sharding import PartitionSpec as P

F32 = jnp.float32
BF16 = jnp.bfloat16
AXES = ("sub", "grp")
CAP = 64
VMEM = pltpu.VMEM
HALF = 64


def dot_nn(left, right):
    return lax.dot_general(left, right, (((1,), (0,)), ((), ())), preferred_element_type=F32)


def dot_nt(left, right):
    return lax.dot_general(left, right, (((1,), (1,)), ((), ())), preferred_element_type=F32)


def low_half(rows):
    return lax.broadcasted_iota(jnp.int32, (rows, 128), 1).astype(BF16) < HALF


def turn(tile):
    return jnp.concatenate([tile[:, HALF:], tile[:, :HALF]], axis=1)


def one_hot(count, index):
    shape = (count, index.shape[1])
    rows = lax.broadcasted_iota(jnp.int32, shape, 0).astype(BF16)
    wanted = jnp.broadcast_to(index.astype(BF16), shape)
    return jnp.where(rows == wanted, jnp.ones(shape, BF16), jnp.zeros(shape, BF16))


def front_kernel(
    live_ref, part_ref, slot_ref, ires_ref, fres_ref, inv_hbm, cpl_hbm,
    cond_ref, out_ref, dest_ref,
    inv_ref, cpl_ref, mark_ref, own_ref, lhs_ref, hot_ref, acc_ref, sem,
):
    subs, vecs, inner = ires_ref.shape
    face = fres_ref.shape[2]
    loads = []
    for s in range(subs):
        one = pltpu.make_async_copy(inv_hbm.at[s], inv_ref.at[s], sem.at[0, s])
        two = pltpu.make_async_copy(cpl_hbm.at[s], cpl_ref.at[s], sem.at[1, s])
        one.start()
        two.start()
        loads.append((one, two))

    width = 256
    sections = out_ref.shape[0]
    chunks = subs * face // width
    row = lax.broadcasted_iota(jnp.int32, (2 * width, width), 0)
    column = lax.broadcasted_iota(jnp.int32, (2 * width, width), 1)
    counter = jnp.where(row - width <= column, 1.0, 0.0).astype(BF16)
    earlier = jnp.zeros((sections, width), BF16)
    for c in range(chunks):
        hot = one_hot(sections, part_ref[:, pl.ds(c * width, width)])
        block = pl.ds(c * sections, sections)
        mark_ref[block, 0:width] = earlier
        mark_ref[block, width:2 * width] = hot
        earlier = earlier + hot
    counted = dot_nn(mark_ref[...], counter).astype(BF16)
    own_ref[...] = jnp.where(mark_ref[:, width:2 * width] > 0, counted, jnp.zeros_like(counted))
    chunk_row = lax.broadcasted_iota(jnp.int32, (chunks, chunks * sections), 0)
    chunk_of = lax.broadcasted_iota(jnp.int32, (chunks, chunks * sections), 1) // sections
    place = dot_nn(jnp.where(chunk_row == chunk_of, 1.0, 0.0).astype(BF16), own_ref[...])
    place = place.astype(jnp.int32) - 1
    for c in range(chunks):
        cols = pl.ds(c * width, width)
        dest_ref[:, cols] = part_ref[:, cols] * CAP + place[c:c + 1]

    groups = sections // 4
    base = groups * vecs
    for s in range(subs):
        loads[s][0].wait()
        loads[s][1].wait()
        pre = dot_nt(ires_ref[s], inv_ref[s]).astype(BF16)
        cond = fres_ref[s].astype(F32) - dot_nt(pre, cpl_ref[s])
        alive = lax.broadcasted_iota(jnp.int32, (vecs, face), 1) < live_ref[s]
        cond = jnp.where(alive, cond, 0.0).astype(BF16)
        cond_ref[s] = cond
        cols = pl.ds(s * face, face)
        dest = dest_ref[:, cols]
        hot_ref[:, cols] = one_hot(256, jnp.bitwise_and(dest, 255))
        group = lax.shift_right_logical(dest, 8).astype(BF16)
        group_all = jnp.broadcast_to(group, (vecs, face))
        for a in range(groups):
            lhs_ref[a * vecs:(a + 1) * vecs, cols] = jnp.where(group_all == a, cond, jnp.zeros_like(cond))
        slot = slot_ref[:, cols]
        mine = one_hot(groups, group)
        high = jnp.broadcast_to(lax.shift_right_logical(slot, 7).astype(BF16), (groups, face))
        low = jnp.broadcast_to(jnp.bitwise_and(slot, 127).astype(BF16), (groups, face))
        lhs_ref[base:base + groups, cols] = mine * high
        lhs_ref[base + groups:base + 2 * groups, cols] = mine * low
        if (s + 1) % 1 == 0:
            span = pl.ds((s + 1 - 1) * face, 1 * face)
            part = dot_nt(lhs_ref[:, span], hot_ref[:, span])
            acc_ref[...] = part if s < 1 else acc_ref[...] + part

    kh = vecs // 2
    mask = low_half(kh)
    mask_wide = low_half(groups)
    first_row = lax.broadcasted_iota(jnp.int32, (8, 128), 0) == 0
    for h in range(2):
        lanes = pl.ds(h * 128, 128)
        slots = []
        for i in range(2):
            value = acc_ref[pl.ds(base + i * groups, groups), lanes].astype(BF16)
            turned = turn(value)
            slots.append((
                jnp.where(mask_wide, value, turned).astype(F32),
                jnp.where(mask_wide, turned, value).astype(F32),
            ))
        for a in range(groups):
            first = acc_ref[pl.ds(a * vecs, kh), lanes].astype(BF16)
            second = turn(acc_ref[pl.ds(a * vecs + kh, kh), lanes].astype(BF16))
            p = 4 * a + 2 * h
            out_ref[p, 0:kh, :] = jnp.where(mask, first, second)
            out_ref[p + 1, 0:kh, :] = jnp.where(mask, second, first)
            for i in range(2):
                both = jnp.where(
                    first_row,
                    jnp.broadcast_to(slots[0][i][a:a + 1], (8, 128)),
                    jnp.broadcast_to(slots[1][i][a:a + 1], (8, 128)),
                )
                out_ref[p + i, kh:kh + 8, :] = both.astype(BF16)


def local_kernel(schur_ref, cond_ref, out_ref):
    out_ref[0] = dot_nt(cond_ref[0], schur_ref[0])


def middle_kernel(recv_ref, inv_ref, out_ref, lhs_ref, hot_ref, high_ref):
    senders = recv_ref.shape[0]
    kh = out_ref.shape[1]
    vecs = 2 * kh
    blocks = inv_ref.shape[0]
    mask = low_half(kh)
    zero = jnp.zeros((kh, 128), BF16)
    for j in range(senders // 2):
        cols = pl.ds(j * 128, 128)
        first = recv_ref[2 * j, 0:kh, :]
        second = recv_ref[2 * j + 1, 0:kh, :]
        data = (jnp.where(mask, first, turn(second)), jnp.where(mask, turn(first), second))
        slots = jnp.where(
            mask[:8],
            recv_ref[2 * j, kh:kh + 8, :],
            recv_ref[2 * j + 1, kh:kh + 8, :],
        )
        hot_ref[:, cols] = one_hot(128, slots[1:2])
        high = jnp.broadcast_to(slots[0:1], (kh, 128))
        high_ref[:, cols] = high
        for c in range(blocks):
            here = high == c
            for i in range(2):
                at = c * vecs + i * kh
                lhs_ref[at:at + kh, cols] = jnp.where(here, data[i], zero)
    summed = dot_nt(lhs_ref[...], hot_ref[...]).astype(BF16)
    solved = jnp.concatenate(
        [dot_nt(summed[c * vecs:(c + 1) * vecs], inv_ref[c]) for c in range(blocks)], axis=0
    ).astype(BF16)
    chunk = 1024
    for n in range(senders * CAP // chunk):
        found = dot_nn(solved, hot_ref[:, pl.ds(n * chunk, chunk)])
        for i in range(chunk // 128):
            lanes = slice(i * 128, (i + 1) * 128)
            j = n * (chunk // 128) + i
            high = high_ref[:, pl.ds(j * 128, 128)]
            parts = []
            for t in range(2):
                part = zero
                for c in range(blocks):
                    at = c * vecs + t * kh
                    part = jnp.where(high == c, found[at:at + kh, lanes].astype(BF16), part)
                parts.append(part)
            out_ref[2 * j] = jnp.where(mask, parts[0], turn(parts[1]))
            out_ref[2 * j + 1] = jnp.where(mask, turn(parts[0]), parts[1])


def back_kernel(
    live_ref, ret_ref, dest_ref, local_ref, ires_ref, inv_hbm, cpl_hbm,
    inner_ref, face_ref,
    inv_ref, cpl_ref, lhs_ref, sem,
):
    subs, vecs, inner = ires_ref.shape
    face = face_ref.shape[2]
    kh = vecs // 2
    loads = []
    for s in range(subs):
        one = pltpu.make_async_copy(inv_hbm.at[s], inv_ref.at[s], sem.at[0, s])
        two = pltpu.make_async_copy(cpl_hbm.at[s], cpl_ref.at[s], sem.at[1, s])
        one.start()
        two.start()
        loads.append((one, two))
    senders = ret_ref.shape[0]
    wide = lhs_ref.shape[1]
    groups = lhs_ref.shape[0] // vecs
    pairs = wide // 128
    mask = low_half(kh)
    for j in range(senders // 2):
        first = ret_ref[2 * j]
        second = ret_ref[2 * j + 1]
        a, i = j // pairs, j % pairs
        lanes = slice(i * 128, (i + 1) * 128)
        lhs_ref[a * vecs:a * vecs + kh, lanes] = jnp.where(mask, first, second)
        lhs_ref[a * vecs + kh:(a + 1) * vecs, lanes] = turn(jnp.where(mask, second, first))
    shift = wide.bit_length() - 1
    for s in range(subs):
        dest = dest_ref[:, pl.ds(s * face, face)]
        group = lax.shift_right_logical(dest, shift)
        within = jnp.bitwise_and(dest, wide - 1)
        hot = jnp.concatenate([one_hot(256, within - 256 * g) for g in range(wide // 256)], axis=0)
        found = dot_nn(lhs_ref[...], hot)
        group_all = jnp.broadcast_to(group, (vecs, face))
        correction = jnp.zeros((vecs, face), F32)
        for a in range(groups):
            correction = jnp.where(group_all == a, found[a * vecs:(a + 1) * vecs], correction)
        alive = lax.broadcasted_iota(jnp.int32, (vecs, face), 1) < live_ref[s]
        update = jnp.where(alive, local_ref[s] + correction, 0.0).astype(BF16)
        face_ref[s] = update
        loads[s][0].wait()
        loads[s][1].wait()
        extended = (ires_ref[s].astype(F32) - dot_nn(update, cpl_ref[s])).astype(BF16)
        inner_ref[s] = dot_nt(extended, inv_ref[s]).astype(BF16)


def vmem(count):
    return [pl.BlockSpec(memory_space=VMEM)] * count


HBM = pl.BlockSpec(memory_space=pltpu.HBM)
SMEM = pl.BlockSpec(memory_space=pltpu.SMEM)


def on_device(
    interior_res,
    interface_res,
    interior_inv,
    coupling,
    schur_inv,
    coarse_inv,
    coarse_part,
    coarse_slot,
    live_count,
):
    subs, vecs, inner = interior_res.shape
    face = interface_res.shape[2]
    rows = subs * face
    sections = lax.axis_size("sub") * lax.axis_size("grp")
    kh = vecs // 2
    groups = sections // 4
    shape = jax.ShapeDtypeStruct

    condensed, outgoing, dest = pl.pallas_call(
        front_kernel,
        name="front",
        out_shape=(
            shape((subs, vecs, face), BF16),
            shape((sections, kh + 8, 128), BF16),
            shape((1, rows), jnp.int32),
        ),
        in_specs=[SMEM] + vmem(4) + [HBM, HBM],
        out_specs=tuple(vmem(3)),
        scratch_shapes=[
            VMEM((subs, inner, inner), BF16),
            VMEM((subs, face, inner), BF16),
            VMEM((rows // 256 * sections, 512), BF16),
            VMEM((rows // 256 * sections, 256), BF16),
            VMEM((groups * (vecs + 2), rows), BF16),
            VMEM((256, rows), BF16),
            VMEM((groups * (vecs + 2), 256), F32),
            pltpu.SemaphoreType.DMA((2, subs)),
        ],
        cost_estimate=pl.CostEstimate(flops=3 * 10**9, bytes_accessed=5 * 10**6, transcendentals=0),
    )(
        live_count, coarse_part.reshape(1, rows), coarse_slot.reshape(1, rows),
        interior_res, interface_res, interior_inv, coupling,
    )

    received = lax.all_to_all(outgoing, AXES, split_axis=0, concat_axis=0, tiled=True)

    local = pl.pallas_call(
        local_kernel,
        name="local",
        compiler_params=pltpu.CompilerParams(vmem_limit_bytes=52 * 2**20),
        grid=(subs,),
        out_shape=shape((subs, vecs, face), F32),
        in_specs=[
            pl.BlockSpec((1, face, face), lambda s: (s, 0, 0)),
            pl.BlockSpec((1, vecs, face), lambda s: (s, 0, 0)),
        ],
        out_specs=pl.BlockSpec((1, vecs, face), lambda s: (s, 0, 0)),
        cost_estimate=pl.CostEstimate(
            flops=2 * rows * vecs * face, bytes_accessed=5 * 10**6, transcendentals=0
        ),
    )(schur_inv, condensed)

    blocks = coarse_inv.shape[0] // lax.axis_size("sub")
    mine = lax.dynamic_slice_in_dim(coarse_inv, lax.axis_index("sub") * blocks, blocks, 0)
    replies = pl.pallas_call(
        middle_kernel,
        name="middle",
        compiler_params=pltpu.CompilerParams(vmem_limit_bytes=24 * 2**20),
        out_shape=shape((sections, kh, 128), BF16),
        in_specs=vmem(2),
        out_specs=vmem(1)[0],
        scratch_shapes=[
            VMEM((blocks * vecs, sections * CAP), BF16),
            VMEM((128, sections * CAP), BF16),
            VMEM((kh, sections * CAP), BF16),
        ],
        cost_estimate=pl.CostEstimate(flops=10**9, bytes_accessed=2 * 10**6, transcendentals=0),
    )(received, mine)

    returned = lax.all_to_all(replies, AXES, split_axis=0, concat_axis=0, tiled=True)

    return pl.pallas_call(
        back_kernel,
        name="back",
        compiler_params=pltpu.CompilerParams(vmem_limit_bytes=52 * 2**20),
        out_shape=(shape((subs, vecs, inner), BF16), shape((subs, vecs, face), BF16)),
        in_specs=[SMEM] + vmem(4) + [HBM, HBM],
        out_specs=tuple(vmem(2)),
        scratch_shapes=[
            VMEM((subs, inner, inner), BF16),
            VMEM((subs, face, inner), BF16),
            VMEM((16 * vecs, sections * CAP // 16), BF16),
            pltpu.SemaphoreType.DMA((2, subs)),
        ],
        cost_estimate=pl.CostEstimate(flops=3 * 10**9, bytes_accessed=6 * 10**6, transcendentals=0),
    )(live_count, returned, dest, local, interior_res, interior_inv, coupling)


def solution(mesh):
    rows = P(AXES)
    in_specs = (rows, rows, rows, rows, rows, P("grp"), rows, rows, rows)
    return jax.shard_map(
        on_device, mesh=mesh, in_specs=in_specs, out_specs=(rows, rows), check_vma=False
    )
```

time: 75.7 us -> 69.5 us (0.918)
  Pallas kernels: 33.4 us -> 27.3 us
  waiting for transfers between devices: 22.7 us -> 24.3 us
  local copies, waits for them, and re-layouts: 2.35 us -> 0.76 us
    pallas_call x3, Pallas kernels: 22.1 us -> 16.1 us  [the longest x1 6.96 us: on_device(): pl.pallas_call(back_kernel, name='back', compiler_params=pltpu.CompilerPa...]
    all_to_all x1, waiting for transfers between devices: 6.95 us -> 7.94 us  [on_device(): lax.all_to_all(replies, AXES, split_axis=0, concat_axis=0, tiled=True)]
    unnamed x6 -> x10, local copies, waits for them, and re-layouts: 1.68 us -> 0.75 us
  transfers between devices with their start and end apart: 2 -> 2, of which waited for: 2 -> 2; matrix products, arithmetic and copies ran while one was open for 1% -> 0% of each run, Pallas kernels for 9% -> 8%
where the time goes in v2:
time: 69.5 us; the launch traced here: 69.1 us
  Pallas kernels  27.3 us (39%)
  waiting for transfers between devices  24.3 us (35%)
  starting transfers between devices  16 us (23%)
  local copies, waits for them, and re-layouts  0.76 us (1%)
  between operations  0.72 us (1%)
    all_to_all x1, waiting for transfers between devices, on_device(): lax.all_to_all(outgoing, AXES, split_axis=0, concat_axis=0, tiled=True)  16.4 us
    all_to_all x1, starting transfers between devices, on_device(): lax.all_to_all(outgoing, AXES, split_axis=0, concat_axis=0, tiled=True)  11.5 us
    pallas_call x1, Pallas kernels, on_device(): pl.pallas_call(front_kernel, name='front', out_shape=(shape((subs, vecs,...  11.2 us
    all_to_all x1, waiting for transfers between devices, on_device(): lax.all_to_all(replies, AXES, split_axis=0, concat_axis=0, tiled=True)  7.94 us
    pallas_call x1, Pallas kernels, on_device(): pl.pallas_call(back_kernel, name='back', compiler_params=pltpu.CompilerPa...  6.96 us
    pallas_call x1, Pallas kernels, on_device(): pl.pallas_call(local_kernel, name='local', compiler_params=pltpu.Compiler...  5.64 us
    all_to_all x1, starting transfers between devices, on_device(): lax.all_to_all(replies, AXES, split_axis=0, concat_axis=0, tiled=True)  4.51 us
    pallas_call x1, Pallas kernels, on_device(): pl.pallas_call(middle_kernel, name='middle', compiler_params=pltpu.Compil...  3.51 us
  transfers between devices with their start and end apart: 2, of which 2 were waited for; matrix products, arithmetic and copies ran while one was open for 0% of the time, Pallas kernels for 8%

profile of v2, /device:TPU:1, one launch (start us, length us, event | category | flops | bytes accessed | tf_op | source)
XLA Modules:
  0.0 69.1 jit_solution(7991906579103779715)
XLA Ops:
  0.6 0.0 copy-start
  0.6 11.2 %front.1 = (bf16[8,32,512]{2,1,0:T(8,128)(2,1)}, bf16[128,24,128]{2,1,0:T(8,128)(2,1)}, s32[1,4096]{1,0:T(1,128)}) custom-call(s32[8]{0:T(128)} %live_ref.3, s32[1,4096]{1,0:T(1,128)} %bitcast.2, s32[1,4096]{1,0:T(1,128)} %bitcast.3, bf16[8,32,256]{2,1,0:T(8,128)(2,1)} %ires_ref.3, bf16[8,32,512]{2,1,0:T(8,128)(2,1)} %fres_ref.1, ...), custom_call_target="tpu_custom_call" | custom-call | flops 3000000000 | bytes 5000000 | tf_op jit(solution)/shard_map/front/pallas_call | solution.py:259
  11.9 11.5 %all-to-all-start = ((bf16[128,24,128]{2,1,0:T(8,128)(2,1)}), bf16[128,24,128]{2,1,0:T(8,128)(2,1)S(1)}, u32[]{:S(2)}, u32[]{:S(2)}) async-start(bf16[128,24,128]{2,1,0:T(8,128)(2,1)} %get-tuple-element.5), calls=%async_computation | async-start | bytes 1572864 | tf_op jit(solution)/shard_map/all_to_all | solution.py:285
  23.4 0.0 copy-done
  23.4 0.0 copy-start.1
  23.4 16.4 %all-to-all-done.recv_ref = bf16[128,24,128]{2,1,0:T(8,128)(2,1)S(1)} async-done(((bf16[128,24,128]{2,1,0:T(8,128)(2,1)}), bf16[128,24,128]{2,1,0:T(8,128)(2,1)S(1)}, u32[]{:S(2)}, u32[]{:S(2)}) %all-to-all-start) | async-done | bytes 786464 | tf_op jit(solution)/shard_map/all_to_all | solution.py:285
  39.8 3.5 %middle.1 = bf16[128,16,128]{2,1,0:T(8,128)(2,1)} custom-call(bf16[128,24,128]{2,1,0:T(8,128)(2,1)S(1)} %all-to-all-done.recv_ref, bf16[4,128,128]{2,1,0:T(8,128)(2,1)S(1)} %constant_dynamic-slice_fusion.inv_ref), custom_call_target="tpu_custom_call" | custom-call | flops 1000000000 | bytes 2000000 | tf_op jit(solution)/shard_map/middle/pallas_call | solution.py:305
  43.3 4.5 %all-to-all-start.1 = ((bf16[128,16,128]{2,1,0:T(8,128)(2,1)}), bf16[128,16,128]{2,1,0:T(8,128)(2,1)S(1)}, u32[]{:S(2)}, u32[]{:S(2)}) async-start(bf16[128,16,128]{2,1,0:T(8,128)(2,1)} %middle.1), calls=%async_computation.1 | async-start | bytes 1048576 | tf_op jit(solution)/shard_map/all_to_all | solution.py:320
  47.8 0.0 copy-done.1
  47.8 0.0 copy-start.2
  47.8 0.0 copy-start.3
  47.8 5.6 %local.1.local_ref = f32[8,32,512]{2,1,0:T(8,128)S(1)} custom-call(bf16[8,512,512]{2,1,0:T(8,128)(2,1)} %schur_ref.1, bf16[8,32,512]{2,1,0:T(8,128)(2,1)S(1)} %copy-done.1), custom_call_target="tpu_custom_call" | custom-call | flops 134217728 | bytes 5000000 | tf_op jit(solution)/shard_map/local/pallas_call | solution.py:287
  53.5 7.9 %all-to-all-done.1.ret_ref = bf16[128,16,128]{2,1,0:T(8,128)(2,1)S(1)} async-done(((bf16[128,16,128]{2,1,0:T(8,128)(2,1)}), bf16[128,16,128]{2,1,0:T(8,128)(2,1)S(1)}, u32[]{:S(2)}, u32[]{:S(2)}) %all-to-all-start.1) | async-done | bytes 524320 | tf_op jit(solution)/shard_map/all_to_all | solution.py:320
  61.4 0.0 copy-done.2
  61.4 0.0 copy-done.3
  61.4 0.0 copy-start.4
  61.4 0.7 %copy-done.4 = s32[1,4096]{1,0:T(1,128)S(1)} copy-done((s32[1,4096]{1,0:T(1,128)S(1)}, s32[1,4096]{1,0:T(1,128)}, u32[]{:S(2)}) %copy-start.4) | copy-done | bytes 16408
  62.2 7.0 %back.1 = (bf16[8,32,256]{2,1,0:T(8,128)(2,1)}, bf16[8,32,512]{2,1,0:T(8,128)(2,1)}) custom-call(s32[8]{0:T(128)S(1)} %copy-done.3, bf16[128,16,128]{2,1,0:T(8,128)(2,1)S(1)} %all-to-all-done.1.ret_ref, s32[1,4096]{1,0:T(1,128)S(1)} %copy-done.4, f32[8,32,512]{2,1,0:T(8,128)S(1)} %local.1.local_ref, bf16[8,32,256]{2,1,0:T(8,128)(2,1)S(1)} %copy-done.2, ...), custom_call_target="tpu_custom_call" | custom-call | flops 3000000000 | bytes 6000000 | tf_op jit(solution)/shard_map/back/pallas_call | solution.py:322
  (1 shorter events, 0.0 us)
Async XLA Ops:
  0.6 22.7 %copy-start = (bf16[64,128,128]{2,1,0:T(8,128)(2,1)S(1)}, bf16[64,128,128]{2,1,0:T(8,128)(2,1)}, u32[]{:S(2)}) copy-start(bf16[64,128,128]{2,1,0:T(8,128)(2,1)} %param.14) | copy-start | bytes 6291460
  11.9 27.9 %all-to-all-start = ((bf16[128,24,128]{2,1,0:T(8,128)(2,1)}), bf16[128,24,128]{2,1,0:T(8,128)(2,1)S(1)}, u32[]{:S(2)}, u32[]{:S(2)}) async-start(bf16[128,24,128]{2,1,0:T(8,128)(2,1)} %get-tuple-element.5), calls=%async_computation | async-start | bytes 1572864 | tf_op jit(solution)/shard_map/all_to_all | solution.py:285
  23.4 24.4 %copy-start.1 = (bf16[8,32,512]{2,1,0:T(8,128)(2,1)S(1)}, bf16[8,32,512]{2,1,0:T(8,128)(2,1)}, u32[]{:S(2)}) copy-start(bf16[8,32,512]{2,1,0:T(8,128)(2,1)} %get-tuple-element.7.cond_ref) | copy-start | bytes 786436
  43.3 18.1 %all-to-all-start.1 = ((bf16[128,16,128]{2,1,0:T(8,128)(2,1)}), bf16[128,16,128]{2,1,0:T(8,128)(2,1)S(1)}, u32[]{:S(2)}, u32[]{:S(2)}) async-start(bf16[128,16,128]{2,1,0:T(8,128)(2,1)} %middle.1), calls=%async_computation.1 | async-start | bytes 1048576 | tf_op jit(solution)/shard_map/all_to_all | solution.py:320
  47.8 13.6 %copy-start.2 = (bf16[8,32,256]{2,1,0:T(8,128)(2,1)S(1)}, bf16[8,32,256]{2,1,0:T(8,128)(2,1)}, u32[]{:S(2)}) copy-start(bf16[8,32,256]{2,1,0:T(8,128)(2,1)} %ires_ref.3) | copy-start | bytes 393220
  47.8 13.6 %copy-start.3 = (s32[8]{0:T(128)S(1)}, s32[8]{0:T(128)}, u32[]{:S(2)}) copy-start(s32[8]{0:T(128)} %live_ref.3) | copy-start | bytes 100
  61.4 0.7 %copy-start.4 = (s32[1,4096]{1,0:T(1,128)S(1)}, s32[1,4096]{1,0:T(1,128)}, u32[]{:S(2)}) copy-start(s32[1,4096]{1,0:T(1,128)} %get-tuple-element.6.dest_ref) | copy-start | bytes 49156

commit v3 on v2

v3 whole, which is shorter than its diff:
```python
import jax
import jax.numpy as jnp
from jax import lax
from jax.experimental import pallas as pl
from jax.experimental.pallas import tpu as pltpu
from jax.sharding import PartitionSpec as P

F32 = jnp.float32
BF16 = jnp.bfloat16
AXES = ("sub", "grp")
CAP = 64
VMEM = pltpu.VMEM
HALF = 64


def dot_nn(left, right):
    return lax.dot_general(left, right, (((1,), (0,)), ((), ())), preferred_element_type=F32)


def dot_nt(left, right):
    return lax.dot_general(left, right, (((1,), (1,)), ((), ())), preferred_element_type=F32)


def low_half(rows):
    return lax.broadcasted_iota(jnp.int32, (rows, 128), 1).astype(BF16) < HALF


def turn(tile):
    return jnp.concatenate([tile[:, HALF:], tile[:, :HALF]], axis=1)


def swap_pair(first, second):
    mask = lax.broadcasted_iota(jnp.int32, first.shape, 1) < HALF
    even = jnp.where(mask, first, pltpu.roll(second, HALF, 1))
    odd = jnp.where(mask, pltpu.roll(first, HALF, 1), second)
    return even, odd


def one_hot(count, index):
    shape = (count, index.shape[1])
    rows = lax.broadcasted_iota(jnp.int32, shape, 0).astype(BF16)
    wanted = jnp.broadcast_to(index.astype(BF16), shape)
    return jnp.where(rows == wanted, jnp.ones(shape, BF16), jnp.zeros(shape, BF16))


def front_kernel(
    live_ref, part_ref, slot_ref, ires_hbm, fres_hbm, inv_hbm, cpl_hbm,
    cond_hbm, out_hbm, dest_ref,
    ires_ref, fres_ref, inv_ref, cpl_ref, mark_ref, own_ref, cond_ref, lhs_ref, hot_ref, mark_slot_ref, place_ref, out_ref,
    sem, res_sem, out_sem, cond_sem,
):
    subs, vecs, inner = ires_ref.shape
    face = fres_ref.shape[2]
    residuals = [
        pltpu.make_async_copy(ires_hbm, ires_ref, res_sem.at[0]),
        pltpu.make_async_copy(fres_hbm, fres_ref, res_sem.at[1]),
    ]
    loads = []
    for copy in residuals:
        copy.start()
    for s in range(subs):
        one = pltpu.make_async_copy(inv_hbm.at[s], inv_ref.at[s], sem.at[0, s])
        two = pltpu.make_async_copy(cpl_hbm.at[s], cpl_ref.at[s], sem.at[1, s])
        loads.append((one, two))
    for i in range(2):
        for s in range(subs):
            loads[s][i].start()

    width = 256
    sections = out_ref.shape[0]
    chunks = subs * face // width
    row = lax.broadcasted_iota(jnp.int32, (2 * width, width), 0)
    column = lax.broadcasted_iota(jnp.int32, (2 * width, width), 1)
    counter = jnp.where(row - width <= column, 1.0, 0.0).astype(BF16)
    earlier = jnp.zeros((sections, width), BF16)
    for c in range(chunks):
        hot = one_hot(sections, part_ref[:, pl.ds(c * width, width)])
        block = pl.ds(c * sections, sections)
        mark_ref[block, 0:width] = earlier
        mark_ref[block, width:2 * width] = hot
        earlier = earlier + hot
    counted = dot_nn(mark_ref[...], counter).astype(BF16)
    own_ref[...] = jnp.where(mark_ref[:, width:2 * width] > 0, counted, jnp.zeros_like(counted))
    chunk_row = lax.broadcasted_iota(jnp.int32, (chunks, chunks * sections), 0)
    chunk_of = lax.broadcasted_iota(jnp.int32, (chunks, chunks * sections), 1) // sections
    place = dot_nn(jnp.where(chunk_row == chunk_of, 1.0, 0.0).astype(BF16), own_ref[...])
    place = place.astype(jnp.int32) - 1
    for c in range(chunks):
        cols = pl.ds(c * width, width)
        dest_ref[:, cols] = part_ref[:, cols] * CAP + place[c:c + 1]
    quads = sections // 4
    for s in range(subs):
        cols = pl.ds(s * face, face)
        dest = dest_ref[:, cols]
        hot_ref[:, cols] = one_hot(256, jnp.bitwise_and(dest, 255))
        mine = one_hot(quads, lax.shift_right_logical(dest, 8))
        slot = slot_ref[:, cols]
        high = lax.shift_right_logical(slot, 7).astype(BF16)
        low = jnp.bitwise_and(slot, 127).astype(BF16)
        mark_slot_ref[0:quads, cols] = mine * jnp.broadcast_to(high, mine.shape)
        mark_slot_ref[quads:2 * quads, cols] = mine * jnp.broadcast_to(low, mine.shape)
    slots = dot_nt(mark_slot_ref[...], hot_ref[...])
    for h in range(2):
        lanes = slice(h * 128, (h + 1) * 128)
        even, odd = swap_pair(slots[0:quads, lanes], slots[quads:2 * quads, lanes])
        place_ref[0:quads, lanes] = even
        place_ref[quads:2 * quads, lanes] = odd

    @pl.when(live_ref[0] >= 0)
    def _():
        for copy in residuals:
            copy.wait()
        for s in range(subs):
            loads[s][0].wait()
        pres = [dot_nt(ires_ref[s], inv_ref[s]).astype(BF16) for s in range(subs)]
        for s in range(subs):
            loads[s][1].wait()
        for s in range(subs):
            cond = fres_ref[s].astype(F32) - dot_nt(pres[s], cpl_ref[s])
            alive = lax.broadcasted_iota(jnp.int32, (vecs, face), 1) < live_ref[s]
            cond_ref[s] = jnp.where(alive, cond, 0.0).astype(BF16)
    keep = pltpu.make_async_copy(cond_ref, cond_hbm, cond_sem)
    keep.start()

    groups = 8
    kh = vecs // 2
    mask = low_half(kh)
    stores = []
    for block in range(quads // groups):
        buf = block % 2
        for s in range(subs):
            cols = pl.ds(s * face, face)
            cond = cond_ref[s]
            group = lax.shift_right_logical(dest_ref[:, cols], 8).astype(BF16) - block * groups
            group_all = jnp.broadcast_to(group, (vecs, face))
            for a in range(groups):
                lhs_ref[buf, a * vecs:(a + 1) * vecs, cols] = jnp.where(
                    group_all == a, cond, jnp.zeros_like(cond)
                )
        acc = dot_nt(lhs_ref[buf], hot_ref[...])
        for h in range(2):
            lanes = slice(h * 128, (h + 1) * 128)
            for a in range(groups):
                first = acc[a * vecs:a * vecs + kh, lanes].astype(BF16)
                second = turn(acc[a * vecs + kh:(a + 1) * vecs, lanes].astype(BF16))
                p = 4 * (block * groups + a) + 2 * h
                out_ref[p, 0:kh, :] = jnp.where(mask, first, second)
                out_ref[p + 1, 0:kh, :] = jnp.where(mask, second, first)
                q = block * groups + a
                for i in range(2):
                    value = place_ref[q + i * quads:q + i * quads + 1, lanes]
                    out_ref[p + i, kh:kh + 8, :] = jnp.broadcast_to(value, (8, 128)).astype(BF16)
        span = pl.ds(block * 4 * groups, 4 * groups)
        store = pltpu.make_async_copy(out_ref.at[span], out_hbm.at[span], out_sem.at[block])
        store.start()
        stores.append(store)
    keep.wait()
    for store in stores:
        store.wait()


def local_kernel(cond_ref, schur_hbm, local_ref, schur_ref, sem):
    subs = cond_ref.shape[0]
    loads = [pltpu.make_async_copy(schur_hbm.at[s], schur_ref.at[s], sem.at[s]) for s in range(subs)]
    for copy in loads:
        copy.start()
    for s in range(subs):
        loads[s].wait()
        local_ref[s] = dot_nt(cond_ref[s], schur_ref[s])


def middle_kernel(recv_ref, inv_ref, out_ref, lhs_ref, hot_ref, high_ref):
    senders = recv_ref.shape[0]
    kh = out_ref.shape[1]
    vecs = 2 * kh
    blocks = inv_ref.shape[0]
    mask = low_half(kh)
    zero = jnp.zeros((kh, 128), BF16)
    for j in range(senders // 2):
        cols = pl.ds(j * 128, 128)
        first = recv_ref[2 * j, 0:kh, :]
        second = recv_ref[2 * j + 1, 0:kh, :]
        data = (jnp.where(mask, first, turn(second)), jnp.where(mask, turn(first), second))
        first = recv_ref[2 * j, kh:kh + 8, :]
        second = recv_ref[2 * j + 1, kh:kh + 8, :]
        hot_ref[:, cols] = one_hot(128, jnp.where(mask[:8], turn(first), second)[0:1])
        high = jnp.broadcast_to(jnp.where(mask[:8], first, turn(second))[0:1], (kh, 128))
        high_ref[:, cols] = high
        for c in range(blocks):
            here = high == c
            for i in range(2):
                at = c * vecs + i * kh
                lhs_ref[at:at + kh, cols] = jnp.where(here, data[i], zero)
    summed = dot_nt(lhs_ref[...], hot_ref[...]).astype(BF16)
    solved = jnp.concatenate(
        [dot_nt(summed[c * vecs:(c + 1) * vecs], inv_ref[c]) for c in range(blocks)], axis=0
    ).astype(BF16)
    chunk = 1024
    for n in range(senders * CAP // chunk):
        found = dot_nn(solved, hot_ref[:, pl.ds(n * chunk, chunk)])
        for i in range(chunk // 128):
            lanes = slice(i * 128, (i + 1) * 128)
            j = n * (chunk // 128) + i
            high = high_ref[:, pl.ds(j * 128, 128)]
            parts = []
            for t in range(2):
                part = zero
                for c in range(blocks):
                    at = c * vecs + t * kh
                    part = jnp.where(high == c, found[at:at + kh, lanes].astype(BF16), part)
                parts.append(part)
            out_ref[2 * j] = jnp.where(mask, parts[0], turn(parts[1]))
            out_ref[2 * j + 1] = jnp.where(mask, turn(parts[0]), parts[1])


def back_kernel(
    live_ref, ret_ref, dest_ref, ires_ref, local_hbm, inv_hbm, cpl_hbm,
    inner_hbm, face_hbm,
    local_ref, inv_ref, cpl_ref, lhs_ref, hot_ref, inner_ref, face_ref, sem, out_sem,
):
    subs, vecs, inner = ires_ref.shape
    face = face_ref.shape[2]
    kh = vecs // 2
    loads = [
        pltpu.make_async_copy(local_hbm, local_ref, sem.at[0]),
        pltpu.make_async_copy(cpl_hbm, cpl_ref, sem.at[1]),
        pltpu.make_async_copy(inv_hbm, inv_ref, sem.at[2]),
    ]
    stores = [
        pltpu.make_async_copy(face_ref, face_hbm, out_sem.at[0]),
        pltpu.make_async_copy(inner_ref, inner_hbm, out_sem.at[1]),
    ]
    for copy in loads:
        copy.start()
    senders = ret_ref.shape[0]
    wide = lhs_ref.shape[1]
    groups = lhs_ref.shape[0] // vecs
    pairs = wide // 128
    mask = low_half(kh)
    for j in range(senders // 2):
        first = ret_ref[2 * j]
        second = ret_ref[2 * j + 1]
        a, i = j // pairs, j % pairs
        lanes = slice(i * 128, (i + 1) * 128)
        lhs_ref[a * vecs:a * vecs + kh, lanes] = jnp.where(mask, first, second)
        lhs_ref[a * vecs + kh:(a + 1) * vecs, lanes] = turn(jnp.where(mask, second, first))
    loads[0].wait()
    shift = wide.bit_length() - 1
    for s in range(subs):
        cols = pl.ds(s * face, face)
        dest = dest_ref[:, cols]
        within = jnp.bitwise_and(dest, wide - 1)
        for g in range(wide // 256):
            hot_ref[s, pl.ds(g * 256, 256), :] = one_hot(256, within - 256 * g)
        found = dot_nn(lhs_ref[...], hot_ref[s])
        group_all = jnp.broadcast_to(lax.shift_right_logical(dest, shift), (vecs, face))
        correction = jnp.zeros((vecs, face), F32)
        for a in range(groups):
            correction = jnp.where(group_all == a, found[a * vecs:(a + 1) * vecs], correction)
        alive = lax.broadcasted_iota(jnp.int32, (vecs, face), 1) < live_ref[s]
        face_ref[s] = jnp.where(alive, local_ref[s] + correction, 0.0).astype(BF16)
    stores[0].start()
    for copy in loads[1:]:
        copy.wait()
    extended = [
        (ires_ref[s].astype(F32) - dot_nn(face_ref[s], cpl_ref[s])).astype(BF16) for s in range(subs)
    ]
    for s in range(subs):
        inner_ref[s] = dot_nt(extended[s], inv_ref[s]).astype(BF16)
    stores[1].start()
    for copy in stores:
        copy.wait()


def vmem(count):
    return [pl.BlockSpec(memory_space=VMEM)] * count


HBM = pl.BlockSpec(memory_space=pltpu.HBM)
SMEM = pl.BlockSpec(memory_space=pltpu.SMEM)


def on_device(
    interior_res,
    interface_res,
    interior_inv,
    coupling,
    schur_inv,
    coarse_inv,
    coarse_part,
    coarse_slot,
    live_count,
):
    subs, vecs, inner = interior_res.shape
    face = interface_res.shape[2]
    rows = subs * face
    sections = lax.axis_size("sub") * lax.axis_size("grp")
    kh = vecs // 2
    groups = sections // 4
    shape = jax.ShapeDtypeStruct

    condensed, outgoing, dest = pl.pallas_call(
        front_kernel,
        name="front",
        out_shape=(
            shape((subs, vecs, face), BF16),
            shape((sections, kh + 8, 128), BF16),
            shape((1, rows), jnp.int32),
        ),
        in_specs=[SMEM] + vmem(2) + [HBM] * 4,
        out_specs=(HBM, HBM, vmem(1)[0]),
        scratch_shapes=[
            VMEM((subs, vecs, inner), BF16),
            VMEM((subs, vecs, face), BF16),
            VMEM((subs, inner, inner), BF16),
            VMEM((subs, face, inner), BF16),
            VMEM((rows // 256 * sections, 512), BF16),
            VMEM((rows // 256 * sections, 256), BF16),
            VMEM((subs, vecs, face), BF16),
            VMEM((2, 8 * vecs, rows), BF16),
            VMEM((256, rows), BF16),
            VMEM((sections // 2, rows), BF16),
            VMEM((sections // 2, 256), F32),
            VMEM((sections, kh + 8, 128), BF16),
            pltpu.SemaphoreType.DMA((2, subs)),
            pltpu.SemaphoreType.DMA((2,)),
            pltpu.SemaphoreType.DMA((sections // 32,)),
            pltpu.SemaphoreType.DMA(()),
        ],
        cost_estimate=pl.CostEstimate(flops=3 * 10**9, bytes_accessed=5 * 10**6, transcendentals=0),
    )(
        live_count, coarse_part.reshape(1, rows), coarse_slot.reshape(1, rows),
        interior_res, interface_res, interior_inv, coupling,
    )

    received = lax.all_to_all(outgoing, AXES, split_axis=0, concat_axis=0, tiled=True)

    local = pl.pallas_call(
        local_kernel,
        name="local",
        compiler_params=pltpu.CompilerParams(vmem_limit_bytes=56 * 2**20),
        out_shape=shape((subs, vecs, face), F32),
        in_specs=vmem(1) + [HBM],
        out_specs=vmem(1)[0],
        scratch_shapes=[VMEM((subs, face, face), BF16), pltpu.SemaphoreType.DMA((subs,))],
        cost_estimate=pl.CostEstimate(
            flops=2 * rows * vecs * face, bytes_accessed=5 * 10**6, transcendentals=0
        ),
    )(condensed, schur_inv)

    blocks = coarse_inv.shape[0] // lax.axis_size("sub")
    mine = lax.dynamic_slice_in_dim(coarse_inv, lax.axis_index("sub") * blocks, blocks, 0)
    replies = pl.pallas_call(
        middle_kernel,
        name="middle",
        compiler_params=pltpu.CompilerParams(vmem_limit_bytes=24 * 2**20),
        out_shape=shape((sections, kh, 128), BF16),
        in_specs=vmem(2),
        out_specs=vmem(1)[0],
        scratch_shapes=[
            VMEM((blocks * vecs, sections * CAP), BF16),
            VMEM((128, sections * CAP), BF16),
            VMEM((kh, sections * CAP), BF16),
        ],
        cost_estimate=pl.CostEstimate(flops=10**9, bytes_accessed=2 * 10**6, transcendentals=0),
    )(received, mine)

    returned = lax.all_to_all(replies, AXES, split_axis=0, concat_axis=0, tiled=True)

    return pl.pallas_call(
        back_kernel,
        name="back",
        compiler_params=pltpu.CompilerParams(vmem_limit_bytes=53 * 2**20),
        out_shape=(shape((subs, vecs, inner), BF16), shape((subs, vecs, face), BF16)),
        in_specs=[SMEM] + vmem(3) + [HBM] * 3,
        out_specs=(HBM, HBM),
        scratch_shapes=[
            VMEM((subs, vecs, face), F32),
            VMEM((subs, inner, inner), BF16),
            VMEM((subs, face, inner), BF16),
            VMEM((16 * vecs, sections * CAP // 16), BF16),
            VMEM((subs, sections * CAP // 16, face), BF16),
            VMEM((subs, vecs, inner), BF16),
            VMEM((subs, vecs, face), BF16),
            pltpu.SemaphoreType.DMA((3,)),
            pltpu.SemaphoreType.DMA((2,)),
        ],
        cost_estimate=pl.CostEstimate(flops=3 * 10**9, bytes_accessed=6 * 10**6, transcendentals=0),
    )(live_count, returned, dest, interior_res, local, interior_inv, coupling)


def solution(mesh):
    rows = P(AXES)
    in_specs = (rows, rows, rows, rows, rows, P("grp"), rows, rows, rows)
    return jax.shard_map(
        on_device, mesh=mesh, in_specs=in_specs, out_specs=(rows, rows), check_vma=False
    )
```

time: 69.5 us -> 65 us (0.935)
  Pallas kernels: 27.3 us -> 22.9 us
  local copies, waits for them, and re-layouts: 0.76 us -> 0.04 us
    pallas_call x1, Pallas kernels: 11.2 us -> 8.7 us  [on_device(): pl.pallas_call(front_kernel, name='front', out_shape=(shape((subs, vecs,...]
    pallas_call x1, Pallas kernels: 6.96 us -> 5.42 us  [on_device(): pl.pallas_call(back_kernel, name='back', compiler_params=pltpu.CompilerPa...]
    unnamed x10 -> x8, local copies, waits for them, and re-layouts: 0.75 us -> 0.03 us
where the time goes in v3:
time: 65 us; the launch traced here: 64.6 us
  waiting for transfers between devices  24.9 us (38%)
  Pallas kernels  22.9 us (35%)
  starting transfers between devices  16 us (25%)
  between operations  0.72 us (1%)
    all_to_all x1, waiting for transfers between devices, on_device(): lax.all_to_all(outgoing, AXES, split_axis=0, concat_axis=0, tiled=True)  16.4 us
    all_to_all x1, starting transfers between devices, on_device(): lax.all_to_all(outgoing, AXES, split_axis=0, concat_axis=0, tiled=True)  11.5 us
    pallas_call x1, Pallas kernels, on_device(): pl.pallas_call(front_kernel, name='front', out_shape=(shape((subs, vecs,...  8.7 us
    all_to_all x1, waiting for transfers between devices, on_device(): lax.all_to_all(replies, AXES, split_axis=0, concat_axis=0, tiled=True)  8.53 us
    pallas_call x1, Pallas kernels, on_device(): pl.pallas_call(back_kernel, name='back', compiler_params=pltpu.CompilerPa...  5.42 us
    pallas_call x1, Pallas kernels, on_device(): pl.pallas_call(local_kernel, name='local', compiler_params=pltpu.Compiler...  5.05 us
    all_to_all x1, starting transfers between devices, on_device(): lax.all_to_all(replies, AXES, split_axis=0, concat_axis=0, tiled=True)  4.52 us
    pallas_call x1, Pallas kernels, on_device(): pl.pallas_call(middle_kernel, name='middle', compiler_params=pltpu.Compil...  3.77 us
  transfers between devices with their start and end apart: 2, of which 2 were waited for; matrix products, arithmetic and copies ran while one was open for 0% of the time, Pallas kernels for 8%

profile of v3, /device:TPU:1, one launch (start us, length us, event | category | flops | bytes accessed | tf_op | source)
XLA Modules:
  0.0 64.6 jit_solution(366382505377938095)
XLA Ops:
  0.6 0.0 copy-start
  0.6 8.7 %front.1 = (bf16[8,32,512]{2,1,0:T(8,128)(2,1)}, bf16[128,24,128]{2,1,0:T(8,128)(2,1)}, s32[1,4096]{1,0:T(1,128)}) custom-call(s32[8]{0:T(128)} %live_ref.3, s32[1,4096]{1,0:T(1,128)} %bitcast.2, s32[1,4096]{1,0:T(1,128)} %bitcast.3, bf16[8,32,256]{2,1,0:T(8,128)(2,1)} %ires_ref.1, bf16[8,32,512]{2,1,0:T(8,128)(2,1)} %fres_hbm.1, ...), custom_call_target="tpu_custom_call" | custom-call | flops 3000000000 | bytes 5000000 | tf_op jit(solution)/shard_map/front/pallas_call | solution.py:302
  9.4 11.5 %all-to-all-start = ((bf16[128,24,128]{2,1,0:T(8,128)(2,1)}), bf16[128,24,128]{2,1,0:T(8,128)(2,1)S(1)}, u32[]{:S(2)}, u32[]{:S(2)}) async-start(bf16[128,24,128]{2,1,0:T(8,128)(2,1)} %get-tuple-element.5), calls=%async_computation | async-start | bytes 1572864 | tf_op jit(solution)/shard_map/all_to_all | solution.py:336
  20.9 0.0 copy-done
  20.9 16.4 %all-to-all-done.recv_ref = bf16[128,24,128]{2,1,0:T(8,128)(2,1)S(1)} async-done(((bf16[128,24,128]{2,1,0:T(8,128)(2,1)}), bf16[128,24,128]{2,1,0:T(8,128)(2,1)S(1)}, u32[]{:S(2)}, u32[]{:S(2)}) %all-to-all-start) | async-done | bytes 786464 | tf_op jit(solution)/shard_map/all_to_all | solution.py:336
  37.3 3.8 %middle.1 = bf16[128,16,128]{2,1,0:T(8,128)(2,1)} custom-call(bf16[128,24,128]{2,1,0:T(8,128)(2,1)S(1)} %all-to-all-done.recv_ref, bf16[4,128,128]{2,1,0:T(8,128)(2,1)S(1)} %constant_dynamic-slice_fusion.inv_ref), custom_call_target="tpu_custom_call" | custom-call | flops 1000000000 | bytes 2000000 | tf_op jit(solution)/shard_map/middle/pallas_call | solution.py:353
  41.0 4.5 %all-to-all-start.1 = ((bf16[128,16,128]{2,1,0:T(8,128)(2,1)}), bf16[128,16,128]{2,1,0:T(8,128)(2,1)S(1)}, u32[]{:S(2)}, u32[]{:S(2)}) async-start(bf16[128,16,128]{2,1,0:T(8,128)(2,1)} %middle.1), calls=%async_computation.1 | async-start | bytes 1048576 | tf_op jit(solution)/shard_map/all_to_all | solution.py:368
  45.6 0.0 copy-start.1
  45.6 0.0 copy-start.2
  45.6 0.0 copy-start.3
  45.6 5.0 %local.1.local_hbm = f32[8,32,512]{2,1,0:T(8,128)} custom-call(bf16[8,32,512]{2,1,0:T(8,128)(2,1)} %get-tuple-element.7.cond_ref, bf16[8,512,512]{2,1,0:T(8,128)(2,1)} %schur_hbm.1), custom_call_target="tpu_custom_call" | custom-call | flops 134217728 | bytes 5000000 | tf_op jit(solution)/shard_map/local/pallas_call | solution.py:338
  50.7 8.5 %all-to-all-done.1.ret_ref = bf16[128,16,128]{2,1,0:T(8,128)(2,1)S(1)} async-done(((bf16[128,16,128]{2,1,0:T(8,128)(2,1)}), bf16[128,16,128]{2,1,0:T(8,128)(2,1)S(1)}, u32[]{:S(2)}, u32[]{:S(2)}) %all-to-all-start.1) | async-done | bytes 524320 | tf_op jit(solution)/shard_map/all_to_all | solution.py:368
  59.2 0.0 copy-done.1
  59.2 0.0 copy-done.2
  59.2 0.0 copy-done.3
  59.2 5.4 %back.1 = (bf16[8,32,256]{2,1,0:T(8,128)(2,1)}, bf16[8,32,512]{2,1,0:T(8,128)(2,1)}) custom-call(s32[8]{0:T(128)S(1)} %copy-done.2, bf16[128,16,128]{2,1,0:T(8,128)(2,1)S(1)} %all-to-all-done.1.ret_ref, s32[1,4096]{1,0:T(1,128)S(1)} %copy-done.3, bf16[8,32,256]{2,1,0:T(8,128)(2,1)S(1)} %copy-done.1, f32[8,32,512]{2,1,0:T(8,128)} %local.1.local_hbm, ...), custom_call_target="tpu_custom_call" | custom-call | flops 3000000000 | bytes 6000000 | tf_op jit(solution)/shard_map/back/pallas_call | solution.py:370
  (1 shorter events, 0.0 us)
Async XLA Ops:
  0.6 20.2 %copy-start = (bf16[64,128,128]{2,1,0:T(8,128)(2,1)S(1)}, bf16[64,128,128]{2,1,0:T(8,128)(2,1)}, u32[]{:S(2)}) copy-start(bf16[64,128,128]{2,1,0:T(8,128)(2,1)} %param.14) | copy-start | bytes 6291460
  9.4 27.9 %all-to-all-start = ((bf16[128,24,128]{2,1,0:T(8,128)(2,1)}), bf16[128,24,128]{2,1,0:T(8,128)(2,1)S(1)}, u32[]{:S(2)}, u32[]{:S(2)}) async-start(bf16[128,24,128]{2,1,0:T(8,128)(2,1)} %get-tuple-element.5), calls=%async_computation | async-start | bytes 1572864 | tf_op jit(solution)/shard_map/all_to_all | solution.py:336
  41.0 18.1 %all-to-all-start.1 = ((bf16[128,16,128]{2,1,0:T(8,128)(2,1)}), bf16[128,16,128]{2,1,0:T(8,128)(2,1)S(1)}, u32[]{:S(2)}, u32[]{:S(2)}) async-start(bf16[128,16,128]{2,1,0:T(8,128)(2,1)} %middle.1), calls=%async_computation.1 | async-start | bytes 1048576 | tf_op jit(solution)/shard_map/all_to_all | solution.py:368
  45.6 13.6 %copy-start.1 = (bf16[8,32,256]{2,1,0:T(8,128)(2,1)S(1)}, bf16[8,32,256]{2,1,0:T(8,128)(2,1)}, u32[]{:S(2)}) copy-start(bf16[8,32,256]{2,1,0:T(8,128)(2,1)} %ires_ref.1) | copy-start | bytes 393220
  45.6 13.6 %copy-start.2 = (s32[8]{0:T(128)S(1)}, s32[8]{0:T(128)}, u32[]{:S(2)}) copy-start(s32[8]{0:T(128)} %live_ref.3) | copy-start | bytes 100
  45.6 13.6 %copy-start.3 = (s32[1,4096]{1,0:T(1,128)S(1)}, s32[1,4096]{1,0:T(1,128)}, u32[]{:S(2)}) copy-start(s32[1,4096]{1,0:T(1,128)} %get-tuple-element.6.dest_ref) | copy-start | bytes 49156

commit v4 on v3

--- a/solution.py
+++ b/solution.py
@@ -67,7 +67,8 @@
             loads[s][i].start()
 
     width = 256
-    sections = out_ref.shape[0]
+    tall = vecs // 2 + 2
+    sections = out_ref.shape[0] // tall
     chunks = subs * face // width
     row = lax.broadcasted_iota(jnp.int32, (2 * width, width), 0)
     column = lax.broadcasted_iota(jnp.int32, (2 * width, width), 1)
@@ -144,13 +145,14 @@
                 first = acc[a * vecs:a * vecs + kh, lanes].astype(BF16)
                 second = turn(acc[a * vecs + kh:(a + 1) * vecs, lanes].astype(BF16))
                 p = 4 * (block * groups + a) + 2 * h
-                out_ref[p, 0:kh, :] = jnp.where(mask, first, second)
-                out_ref[p + 1, 0:kh, :] = jnp.where(mask, second, first)
+                out_ref[p * tall:p * tall + kh, :] = jnp.where(mask, first, second)
+                out_ref[(p + 1) * tall:(p + 1) * tall + kh, :] = jnp.where(mask, second, first)
                 q = block * groups + a
                 for i in range(2):
                     value = place_ref[q + i * quads:q + i * quads + 1, lanes]
-                    out_ref[p + i, kh:kh + 8, :] = jnp.broadcast_to(value, (8, 128)).astype(BF16)
-        span = pl.ds(block * 4 * groups, 4 * groups)
+                    at = (p + i) * tall + kh
+                    out_ref[at:at + 2, :] = jnp.broadcast_to(value, (2, 128)).astype(BF16)
+        span = pl.ds(block * 4 * groups * tall, 4 * groups * tall)
         store = pltpu.make_async_copy(out_ref.at[span], out_hbm.at[span], out_sem.at[block])
         store.start()
         stores.append(store)
@@ -170,21 +172,22 @@
 
 
 def middle_kernel(recv_ref, inv_ref, out_ref, lhs_ref, hot_ref, high_ref):
-    senders = recv_ref.shape[0]
-    kh = out_ref.shape[1]
+    senders, kh = out_ref.shape[:2]
+    tall = kh + 2
     vecs = 2 * kh
     blocks = inv_ref.shape[0]
     mask = low_half(kh)
     zero = jnp.zeros((kh, 128), BF16)
     for j in range(senders // 2):
         cols = pl.ds(j * 128, 128)
-        first = recv_ref[2 * j, 0:kh, :]
-        second = recv_ref[2 * j + 1, 0:kh, :]
+        at, then = 2 * j * tall, (2 * j + 1) * tall
+        first = recv_ref[at:at + kh, :]
+        second = recv_ref[then:then + kh, :]
         data = (jnp.where(mask, first, turn(second)), jnp.where(mask, turn(first), second))
-        first = recv_ref[2 * j, kh:kh + 8, :]
-        second = recv_ref[2 * j + 1, kh:kh + 8, :]
-        hot_ref[:, cols] = one_hot(128, jnp.where(mask[:8], turn(first), second)[0:1])
-        high = jnp.broadcast_to(jnp.where(mask[:8], first, turn(second))[0:1], (kh, 128))
+        first = recv_ref[at + kh:at + tall, :]
+        second = recv_ref[then + kh:then + tall, :]
+        hot_ref[:, cols] = one_hot(128, jnp.where(mask[:2], turn(first), second)[0:1])
+        high = jnp.broadcast_to(jnp.where(mask[:2], first, turn(second))[0:1], (kh, 128))
         high_ref[:, cols] = high
         for c in range(blocks):
             here = high == c
@@ -304,7 +307,7 @@
         name="front",
         out_shape=(
             shape((subs, vecs, face), BF16),
-            shape((sections, kh + 8, 128), BF16),
+            shape((sections * (kh + 2), 128), BF16),
             shape((1, rows), jnp.int32),
         ),
         in_specs=[SMEM] + vmem(2) + [HBM] * 4,
@@ -321,7 +324,7 @@
             VMEM((256, rows), BF16),
             VMEM((sections // 2, rows), BF16),
             VMEM((sections // 2, 256), F32),
-            VMEM((sections, kh + 8, 128), BF16),
+            VMEM((sections * (kh + 2), 128), BF16),
             pltpu.SemaphoreType.DMA((2, subs)),
             pltpu.SemaphoreType.DMA((2,)),
             pltpu.SemaphoreType.DMA((sections // 32,)),
@@ -333,7 +336,9 @@
         interior_res, interface_res, interior_inv, coupling,
     )
 
-    received = lax.all_to_all(outgoing, AXES, split_axis=0, concat_axis=0, tiled=True)
+    paired = outgoing.reshape(sections * (kh + 2) // 2, 2, 128)
+    received = lax.all_to_all(paired, AXES, split_axis=0, concat_axis=0, tiled=True)
+    received = received.reshape(sections * (kh + 2), 128)
 
     local = pl.pallas_call(
         local_kernel,

time: 65 us -> 62.9 us (0.968)
  waiting for transfers between devices: 24.9 us -> 22.8 us
    all_to_all x1, waiting for transfers between devices: 16.4 us -> 14.3 us  [on_device(): lax.all_to_all(paired, AXES, split_axis=0, concat_axis=0, tiled=True)]
where the time goes in v4:
time: 62.9 us; the launch traced here: 62.6 us
  Pallas kernels  23 us (37%)
  waiting for transfers between devices  22.8 us (36%)
  starting transfers between devices  16.1 us (26%)
  between operations  0.72 us (1%)
    all_to_all x1, waiting for transfers between devices, on_device(): lax.all_to_all(paired, AXES, split_axis=0, concat_axis=0, tiled=True)  14.3 us
    all_to_all x1, starting transfers between devices, on_device(): lax.all_to_all(paired, AXES, split_axis=0, concat_axis=0, tiled=True)  11.5 us
    pallas_call x1, Pallas kernels, on_device(): pl.pallas_call(front_kernel, name='front', out_shape=(shape((subs, vecs,...  8.68 us
    all_to_all x1, waiting for transfers between devices, on_device(): lax.all_to_all(replies, AXES, split_axis=0, concat_axis=0, tiled=True)  8.52 us
    pallas_call x1, Pallas kernels, on_device(): pl.pallas_call(back_kernel, name='back', compiler_params=pltpu.CompilerPa...  5.42 us
    pallas_call x1, Pallas kernels, on_device(): pl.pallas_call(local_kernel, name='local', compiler_params=pltpu.Compiler...  5.04 us
    all_to_all x1, starting transfers between devices, on_device(): lax.all_to_all(replies, AXES, split_axis=0, concat_axis=0, tiled=True)  4.58 us
    pallas_call x1, Pallas kernels, on_device(): pl.pallas_call(middle_kernel, name='middle', compiler_params=pltpu.Compil...  3.86 us
  transfers between devices with their start and end apart: 2, of which 2 were waited for; matrix products, arithmetic and copies ran while one was open for 0% of the time, Pallas kernels for 8%

profile of v4, /device:TPU:1, one launch (start us, length us, event | category | flops | bytes accessed | tf_op | source)
XLA Modules:
  0.0 62.6 jit_solution(1533394380760811705)
XLA Ops:
  0.6 0.0 copy-start
  0.6 8.7 %front.1 = (bf16[8,32,512]{2,1,0:T(8,128)(2,1)}, bf16[2304,128]{1,0:T(8,128)(2,1)}, s32[1,4096]{1,0:T(1,128)}) custom-call(s32[8]{0:T(128)} %live_ref.3, s32[1,4096]{1,0:T(1,128)} %bitcast.6, s32[1,4096]{1,0:T(1,128)} %bitcast.7, bf16[8,32,256]{2,1,0:T(8,128)(2,1)} %ires_ref.1, bf16[8,32,512]{2,1,0:T(8,128)(2,1)} %fres_hbm.1, bf16[8,256,256]{2,1,0:T(8,128)(2,1)} %inv_hbm.3, ...), custom_call_target="tpu_custom_call" | custom-call | flops 3000000000 | bytes 5000000 | tf_op jit(solution)/shard_map/front/pallas_call | solution.py:305
  9.3 11.5 %all-to-all-start = ((bf16[1152,2,128]{2,1,0:T(2,128)(2,1)}), bf16[1152,2,128]{2,1,0:T(2,128)(2,1)S(1)}, u32[]{:S(2)}, u32[]{:S(2)}) async-start(bf16[1152,2,128]{2,1,0:T(2,128)(2,1)} %bitcast.5), calls=%async_computation | async-start | bytes 1179648 | tf_op jit(solution)/shard_map/all_to_all | solution.py:340
  20.8 0.0 copy-done
  20.9 14.3 %all-to-all-done = bf16[1152,2,128]{2,1,0:T(2,128)(2,1)S(1)} async-done(((bf16[1152,2,128]{2,1,0:T(2,128)(2,1)}), bf16[1152,2,128]{2,1,0:T(2,128)(2,1)S(1)}, u32[]{:S(2)}, u32[]{:S(2)}) %all-to-all-start) | async-done | bytes 589856 | tf_op jit(solution)/shard_map/all_to_all | solution.py:340
  35.1 3.9 %middle.1 = bf16[128,16,128]{2,1,0:T(8,128)(2,1)} custom-call(bf16[2304,128]{1,0:T(8,128)(2,1)S(1)} %bitcast.4, bf16[4,128,128]{2,1,0:T(8,128)(2,1)S(1)} %constant_dynamic-slice_fusion.inv_ref), custom_call_target="tpu_custom_call" | custom-call | flops 1000000000 | bytes 2000000 | tf_op jit(solution)/shard_map/middle/pallas_call | solution.py:358
  39.0 4.6 %all-to-all-start.1 = ((bf16[128,16,128]{2,1,0:T(8,128)(2,1)}), bf16[128,16,128]{2,1,0:T(8,128)(2,1)S(1)}, u32[]{:S(2)}, u32[]{:S(2)}) async-start(bf16[128,16,128]{2,1,0:T(8,128)(2,1)} %middle.1), calls=%async_computation.1 | async-start | bytes 1048576 | tf_op jit(solution)/shard_map/all_to_all | solution.py:373
  43.6 0.0 copy-start.1
  43.6 0.0 copy-start.2
  43.6 0.0 copy-start.3
  43.6 5.0 %local.1.local_hbm = f32[8,32,512]{2,1,0:T(8,128)} custom-call(bf16[8,32,512]{2,1,0:T(8,128)(2,1)} %get-tuple-element.7.cond_ref, bf16[8,512,512]{2,1,0:T(8,128)(2,1)} %schur_hbm.1), custom_call_target="tpu_custom_call" | custom-call | flops 134217728 | bytes 5000000 | tf_op jit(solution)/shard_map/local/pallas_call | solution.py:343
  48.7 8.5 %all-to-all-done.1.ret_ref = bf16[128,16,128]{2,1,0:T(8,128)(2,1)S(1)} async-done(((bf16[128,16,128]{2,1,0:T(8,128)(2,1)}), bf16[128,16,128]{2,1,0:T(8,128)(2,1)S(1)}, u32[]{:S(2)}, u32[]{:S(2)}) %all-to-all-start.1) | async-done | bytes 524320 | tf_op jit(solution)/shard_map/all_to_all | solution.py:373
  57.2 0.0 copy-done.1
  57.2 0.0 copy-done.2
  57.2 0.0 copy-done.3
  57.2 5.4 %back.1 = (bf16[8,32,256]{2,1,0:T(8,128)(2,1)}, bf16[8,32,512]{2,1,0:T(8,128)(2,1)}) custom-call(s32[8]{0:T(128)S(1)} %copy-done.2, bf16[128,16,128]{2,1,0:T(8,128)(2,1)S(1)} %all-to-all-done.1.ret_ref, s32[1,4096]{1,0:T(1,128)S(1)} %copy-done.3, bf16[8,32,256]{2,1,0:T(8,128)(2,1)S(1)} %copy-done.1, f32[8,32,512]{2,1,0:T(8,128)} %local.1.local_hbm, ...), custom_call_target="tpu_custom_call" | custom-call | flops 3000000000 | bytes 6000000 | tf_op jit(solution)/shard_map/back/pallas_call | solution.py:375
  (1 shorter events, 0.0 us)
Async XLA Ops:
  0.6 20.2 %copy-start = (bf16[64,128,128]{2,1,0:T(8,128)(2,1)S(1)}, bf16[64,128,128]{2,1,0:T(8,128)(2,1)}, u32[]{:S(2)}) copy-start(bf16[64,128,128]{2,1,0:T(8,128)(2,1)} %param.14) | copy-start | bytes 6291460
  9.3 25.8 %all-to-all-start = ((bf16[1152,2,128]{2,1,0:T(2,128)(2,1)}), bf16[1152,2,128]{2,1,0:T(2,128)(2,1)S(1)}, u32[]{:S(2)}, u32[]{:S(2)}) async-start(bf16[1152,2,128]{2,1,0:T(2,128)(2,1)} %bitcast.5), calls=%async_computation | async-start | bytes 1179648 | tf_op jit(solution)/shard_map/all_to_all | solution.py:340
  39.0 18.2 %all-to-all-start.1 = ((bf16[128,16,128]{2,1,0:T(8,128)(2,1)}), bf16[128,16,128]{2,1,0:T(8,128)(2,1)S(1)}, u32[]{:S(2)}, u32[]{:S(2)}) async-start(bf16[128,16,128]{2,1,0:T(8,128)(2,1)} %middle.1), calls=%async_computation.1 | async-start | bytes 1048576 | tf_op jit(solution)/shard_map/all_to_all | solution.py:373
  43.6 13.6 %copy-start.1 = (bf16[8,32,256]{2,1,0:T(8,128)(2,1)S(1)}, bf16[8,32,256]{2,1,0:T(8,128)(2,1)}, u32[]{:S(2)}) copy-start(bf16[8,32,256]{2,1,0:T(8,128)(2,1)} %ires_ref.1) | copy-start | bytes 393220
  43.6 13.6 %copy-start.2 = (s32[8]{0:T(128)S(1)}, s32[8]{0:T(128)}, u32[]{:S(2)}) copy-start(s32[8]{0:T(128)} %live_ref.3) | copy-start | bytes 100
  43.6 13.6 %copy-start.3 = (s32[1,4096]{1,0:T(1,128)S(1)}, s32[1,4096]{1,0:T(1,128)}, u32[]{:S(2)}) copy-start(s32[1,4096]{1,0:T(1,128)} %get-tuple-element.6.dest_ref) | copy-start | bytes 49156

commit v5 on v4

--- a/solution.py
+++ b/solution.py
@@ -45,9 +45,9 @@
 
 def front_kernel(
     live_ref, part_ref, slot_ref, ires_hbm, fres_hbm, inv_hbm, cpl_hbm,
-    cond_hbm, out_hbm, dest_ref,
-    ires_ref, fres_ref, inv_ref, cpl_ref, mark_ref, own_ref, cond_ref, lhs_ref, hot_ref, mark_slot_ref, place_ref, out_ref,
-    sem, res_sem, out_sem, cond_sem,
+    cond_hbm, out_hbm, dest_hbm,
+    ires_ref, fres_ref, inv_ref, cpl_ref, mark_ref, own_ref, cond_ref, lhs_ref, hot_ref, mark_slot_ref, place_ref, out_ref, dest_ref,
+    sem, res_sem, out_sem, keep_sem,
 ):
     subs, vecs, inner = ires_ref.shape
     face = fres_ref.shape[2]
@@ -70,18 +70,19 @@
     tall = vecs // 2 + 2
     sections = out_ref.shape[0] // tall
     chunks = subs * face // width
-    row = lax.broadcasted_iota(jnp.int32, (2 * width, width), 0)
-    column = lax.broadcasted_iota(jnp.int32, (2 * width, width), 1)
-    counter = jnp.where(row - width <= column, 1.0, 0.0).astype(BF16)
-    earlier = jnp.zeros((sections, width), BF16)
+    row = lax.broadcasted_iota(jnp.int32, (width, width), 0)
+    column = lax.broadcasted_iota(jnp.int32, (width, width), 1)
+    counter = jnp.where(row <= column, 1.0, 0.0).astype(BF16)
     for c in range(chunks):
-        hot = one_hot(sections, part_ref[:, pl.ds(c * width, width)])
-        block = pl.ds(c * sections, sections)
-        mark_ref[block, 0:width] = earlier
-        mark_ref[block, width:2 * width] = hot
-        earlier = earlier + hot
-    counted = dot_nn(mark_ref[...], counter).astype(BF16)
-    own_ref[...] = jnp.where(mark_ref[:, width:2 * width] > 0, counted, jnp.zeros_like(counted))
+        mark_ref[pl.ds(c * sections, sections), :] = one_hot(sections, part_ref[:, pl.ds(c * width, width)])
+    counted = dot_nn(mark_ref[...], counter)
+    run = jnp.zeros((sections, width), F32)
+    for c in range(chunks):
+        block = slice(c * sections, (c + 1) * sections)
+        within = counted[block]
+        total = (within + run).astype(BF16)
+        own_ref[block, :] = jnp.where(mark_ref[block, :] > 0, total, jnp.zeros_like(total))
+        run = run + jnp.broadcast_to(within[:, width - 1:width], (sections, width))
     chunk_row = lax.broadcasted_iota(jnp.int32, (chunks, chunks * sections), 0)
     chunk_of = lax.broadcasted_iota(jnp.int32, (chunks, chunks * sections), 1) // sections
     place = dot_nn(jnp.where(chunk_row == chunk_of, 1.0, 0.0).astype(BF16), own_ref[...])
@@ -90,22 +91,6 @@
         cols = pl.ds(c * width, width)
         dest_ref[:, cols] = part_ref[:, cols] * CAP + place[c:c + 1]
     quads = sections // 4
-    for s in range(subs):
-        cols = pl.ds(s * face, face)
-        dest = dest_ref[:, cols]
-        hot_ref[:, cols] = one_hot(256, jnp.bitwise_and(dest, 255))
-        mine = one_hot(quads, lax.shift_right_logical(dest, 8))
-        slot = slot_ref[:, cols]
-        high = lax.shift_right_logical(slot, 7).astype(BF16)
-        low = jnp.bitwise_and(slot, 127).astype(BF16)
-        mark_slot_ref[0:quads, cols] = mine * jnp.broadcast_to(high, mine.shape)
-        mark_slot_ref[quads:2 * quads, cols] = mine * jnp.broadcast_to(low, mine.shape)
-    slots = dot_nt(mark_slot_ref[...], hot_ref[...])
-    for h in range(2):
-        lanes = slice(h * 128, (h + 1) * 128)
-        even, odd = swap_pair(slots[0:quads, lanes], slots[quads:2 * quads, lanes])
-        place_ref[0:quads, lanes] = even
-        place_ref[quads:2 * quads, lanes] = odd
 
     @pl.when(live_ref[0] >= 0)
     def _():
@@ -113,15 +98,35 @@
             copy.wait()
         for s in range(subs):
             loads[s][0].wait()
+        for s in range(subs):
+            loads[s][1].wait()
+        for s in range(subs):
+            cols = pl.ds(s * face, face)
+            dest = dest_ref[:, cols]
+            hot_ref[:, cols] = one_hot(256, jnp.bitwise_and(dest, 255))
+            mine = one_hot(quads, lax.shift_right_logical(dest, 8))
+            slot = slot_ref[:, cols]
+            high = lax.shift_right_logical(slot, 7).astype(BF16)
+            low = jnp.bitwise_and(slot, 127).astype(BF16)
+            mark_slot_ref[0:quads, cols] = mine * jnp.broadcast_to(high, mine.shape)
+            mark_slot_ref[quads:2 * quads, cols] = mine * jnp.broadcast_to(low, mine.shape)
+        slots = dot_nt(mark_slot_ref[...], hot_ref[...])
+        for h in range(2):
+            lanes = slice(h * 128, (h + 1) * 128)
+            even, odd = swap_pair(slots[0:quads, lanes], slots[quads:2 * quads, lanes])
+            place_ref[0:quads, lanes] = even
+            place_ref[quads:2 * quads, lanes] = odd
         pres = [dot_nt(ires_ref[s], inv_ref[s]).astype(BF16) for s in range(subs)]
-        for s in range(subs):
-            loads[s][1].wait()
         for s in range(subs):
             cond = fres_ref[s].astype(F32) - dot_nt(pres[s], cpl_ref[s])
             alive = lax.broadcasted_iota(jnp.int32, (vecs, face), 1) < live_ref[s]
             cond_ref[s] = jnp.where(alive, cond, 0.0).astype(BF16)
-    keep = pltpu.make_async_copy(cond_ref, cond_hbm, cond_sem)
-    keep.start()
+    keeps = [
+        pltpu.make_async_copy(cond_ref, cond_hbm, keep_sem.at[0]),
+        pltpu.make_async_copy(dest_ref, dest_hbm, keep_sem.at[1]),
+    ]
+    for copy in keeps:
+        copy.start()
 
     groups = 8
     kh = vecs // 2
@@ -156,9 +161,8 @@
         store = pltpu.make_async_copy(out_ref.at[span], out_hbm.at[span], out_sem.at[block])
         store.start()
         stores.append(store)
-    keep.wait()
-    for store in stores:
-        store.wait()
+    for copy in keeps + stores:
+        copy.wait()
 
 
 def local_kernel(cond_ref, schur_hbm, local_ref, schur_ref, sem):
@@ -171,7 +175,7 @@
         local_ref[s] = dot_nt(cond_ref[s], schur_ref[s])
 
 
-def middle_kernel(recv_ref, inv_ref, out_ref, lhs_ref, hot_ref, high_ref):
+def middle_kernel(recv_ref, inv_ref, out_hbm, lhs_ref, hot_ref, high_ref, out_ref, sem):
     senders, kh = out_ref.shape[:2]
     tall = kh + 2
     vecs = 2 * kh
@@ -199,6 +203,7 @@
         [dot_nt(summed[c * vecs:(c + 1) * vecs], inv_ref[c]) for c in range(blocks)], axis=0
     ).astype(BF16)
     chunk = 1024
+    stores = []
     for n in range(senders * CAP // chunk):
         found = dot_nn(solved, hot_ref[:, pl.ds(n * chunk, chunk)])
         for i in range(chunk // 128):
@@ -214,6 +219,12 @@
                 parts.append(part)
             out_ref[2 * j] = jnp.where(mask, parts[0], turn(parts[1]))
             out_ref[2 * j + 1] = jnp.where(mask, turn(parts[0]), parts[1])
+        span = pl.ds(n * (chunk // CAP), chunk // CAP)
+        store = pltpu.make_async_copy(out_ref.at[span], out_hbm.at[span], sem.at[n])
+        store.start()
+        stores.append(store)
+    for store in stores:
+        store.wait()
 
 
 def back_kernel(
@@ -311,13 +322,13 @@
             shape((1, rows), jnp.int32),
         ),
         in_specs=[SMEM] + vmem(2) + [HBM] * 4,
-        out_specs=(HBM, HBM, vmem(1)[0]),
+        out_specs=(HBM, HBM, HBM),
         scratch_shapes=[
             VMEM((subs, vecs, inner), BF16),
             VMEM((subs, vecs, face), BF16),
             VMEM((subs, inner, inner), BF16),
             VMEM((subs, face, inner), BF16),
-            VMEM((rows // 256 * sections, 512), BF16),
+            VMEM((rows // 256 * sections, 256), BF16),
             VMEM((rows // 256 * sections, 256), BF16),
             VMEM((subs, vecs, face), BF16),
             VMEM((2, 8 * vecs, rows), BF16),
@@ -325,10 +336,11 @@
             VMEM((sections // 2, rows), BF16),
             VMEM((sections // 2, 256), F32),
             VMEM((sections * (kh + 2), 128), BF16),
+            VMEM((1, rows), jnp.int32),
             pltpu.SemaphoreType.DMA((2, subs)),
             pltpu.SemaphoreType.DMA((2,)),
             pltpu.SemaphoreType.DMA((sections // 32,)),
-            pltpu.SemaphoreType.DMA(()),
+            pltpu.SemaphoreType.DMA((2,)),
         ],
         cost_estimate=pl.CostEstimate(flops=3 * 10**9, bytes_accessed=5 * 10**6, transcendentals=0),
     )(
@@ -361,11 +373,13 @@
         compiler_params=pltpu.CompilerParams(vmem_limit_bytes=24 * 2**20),
         out_shape=shape((sections, kh, 128), BF16),
         in_specs=vmem(2),
-        out_specs=vmem(1)[0],
+        out_specs=HBM,
         scratch_shapes=[
             VMEM((blocks * vecs, sections * CAP), BF16),
             VMEM((128, sections * CAP), BF16),
             VMEM((kh, sections * CAP), BF16),
+            VMEM((sections, kh, 128), BF16),
+            pltpu.SemaphoreType.DMA((sections * CAP // 1024,)),
         ],
         cost_estimate=pl.CostEstimate(flops=10**9, bytes_accessed=2 * 10**6, transcendentals=0),
     )(received, mine)

time: 62.9 us -> 62 us (0.986)
  Pallas kernels: 23 us -> 22.1 us
    pallas_call x1, Pallas kernels: 8.68 us -> 7.86 us  [on_device(): pl.pallas_call(front_kernel, name='front', out_shape=(shape((subs, vecs,...]
where the time goes in v5:
time: 62 us; the launch traced here: 61.7 us
  waiting for transfers between devices  22.8 us (37%)
  Pallas kernels  22.1 us (36%)
  starting transfers between devices  16.1 us (26%)
  between operations  0.73 us (1%)
    all_to_all x1, waiting for transfers between devices, on_device(): lax.all_to_all(paired, AXES, split_axis=0, concat_axis=0, tiled=True)  14.3 us
    all_to_all x1, starting transfers between devices, on_device(): lax.all_to_all(paired, AXES, split_axis=0, concat_axis=0, tiled=True)  11.5 us
    all_to_all x1, waiting for transfers between devices, on_device(): lax.all_to_all(replies, AXES, split_axis=0, concat_axis=0, tiled=True)  8.52 us
    pallas_call x1, Pallas kernels, on_device(): pl.pallas_call(front_kernel, name='front', out_shape=(shape((subs, vecs,...  7.86 us
    pallas_call x1, Pallas kernels, on_device(): pl.pallas_call(back_kernel, name='back', compiler_params=pltpu.CompilerPa...  5.42 us
    pallas_call x1, Pallas kernels, on_device(): pl.pallas_call(local_kernel, name='local', compiler_params=pltpu.Compiler...  5.04 us
    all_to_all x1, starting transfers between devices, on_device(): lax.all_to_all(replies, AXES, split_axis=0, concat_axis=0, tiled=True)  4.58 us
    pallas_call x1, Pallas kernels, on_device(): pl.pallas_call(middle_kernel, name='middle', compiler_params=pltpu.Compil...  3.75 us
  transfers between devices with their start and end apart: 2, of which 2 were waited for; matrix products, arithmetic and copies ran while one was open for 0% of the time, Pallas kernels for 8%

profile of v5, /device:TPU:1, one launch (start us, length us, event | category | flops | bytes accessed | tf_op | source)
XLA Modules:
  0.0 61.7 jit_solution(17689938666272864198)
XLA Ops:
  0.6 0.0 copy-start
  0.6 7.9 %front.1 = (bf16[8,32,512]{2,1,0:T(8,128)(2,1)}, bf16[2304,128]{1,0:T(8,128)(2,1)}, s32[1,4096]{1,0:T(1,128)}) custom-call(s32[8]{0:T(128)} %live_ref.3, s32[1,4096]{1,0:T(1,128)} %bitcast.6, s32[1,4096]{1,0:T(1,128)} %bitcast.7, bf16[8,32,256]{2,1,0:T(8,128)(2,1)} %ires_ref.1, bf16[8,32,512]{2,1,0:T(8,128)(2,1)} %fres_hbm.1, bf16[8,256,256]{2,1,0:T(8,128)(2,1)} %inv_hbm.3, ...), custom_call_target="tpu_custom_call" | custom-call | flops 3000000000 | bytes 5000000 | tf_op jit(solution)/shard_map/front/pallas_call | solution.py:316
  8.5 11.5 %all-to-all-start = ((bf16[1152,2,128]{2,1,0:T(2,128)(2,1)}), bf16[1152,2,128]{2,1,0:T(2,128)(2,1)S(1)}, u32[]{:S(2)}, u32[]{:S(2)}) async-start(bf16[1152,2,128]{2,1,0:T(2,128)(2,1)} %bitcast.5), calls=%async_computation | async-start | bytes 1179648 | tf_op jit(solution)/shard_map/all_to_all | solution.py:352
  20.0 0.0 copy-done
  20.1 14.3 %all-to-all-done = bf16[1152,2,128]{2,1,0:T(2,128)(2,1)S(1)} async-done(((bf16[1152,2,128]{2,1,0:T(2,128)(2,1)}), bf16[1152,2,128]{2,1,0:T(2,128)(2,1)S(1)}, u32[]{:S(2)}, u32[]{:S(2)}) %all-to-all-start) | async-done | bytes 589856 | tf_op jit(solution)/shard_map/all_to_all | solution.py:352
  34.3 3.7 %middle.1 = bf16[128,16,128]{2,1,0:T(8,128)(2,1)} custom-call(bf16[2304,128]{1,0:T(8,128)(2,1)S(1)} %bitcast.4, bf16[4,128,128]{2,1,0:T(8,128)(2,1)S(1)} %constant_dynamic-slice_fusion.inv_ref), custom_call_target="tpu_custom_call" | custom-call | flops 1000000000 | bytes 2000000 | tf_op jit(solution)/shard_map/middle/pallas_call | solution.py:370
  38.1 4.6 %all-to-all-start.1 = ((bf16[128,16,128]{2,1,0:T(8,128)(2,1)}), bf16[128,16,128]{2,1,0:T(8,128)(2,1)S(1)}, u32[]{:S(2)}, u32[]{:S(2)}) async-start(bf16[128,16,128]{2,1,0:T(8,128)(2,1)} %middle.1), calls=%async_computation.1 | async-start | bytes 1048576 | tf_op jit(solution)/shard_map/all_to_all | solution.py:387
  42.7 0.0 copy-start.1
  42.7 0.0 copy-start.2
  42.7 0.0 copy-start.3
  42.7 5.0 %local.1.local_hbm = f32[8,32,512]{2,1,0:T(8,128)} custom-call(bf16[8,32,512]{2,1,0:T(8,128)(2,1)} %get-tuple-element.7.cond_ref, bf16[8,512,512]{2,1,0:T(8,128)(2,1)} %schur_hbm.1), custom_call_target="tpu_custom_call" | custom-call | flops 134217728 | bytes 5000000 | tf_op jit(solution)/shard_map/local/pallas_call | solution.py:355
  47.8 8.5 %all-to-all-done.1.ret_ref = bf16[128,16,128]{2,1,0:T(8,128)(2,1)S(1)} async-done(((bf16[128,16,128]{2,1,0:T(8,128)(2,1)}), bf16[128,16,128]{2,1,0:T(8,128)(2,1)S(1)}, u32[]{:S(2)}, u32[]{:S(2)}) %all-to-all-start.1) | async-done | bytes 524320 | tf_op jit(solution)/shard_map/all_to_all | solution.py:387
  56.3 0.0 copy-done.1
  56.3 0.0 copy-done.2
  56.3 0.0 copy-done.3
  56.3 5.4 %back.1 = (bf16[8,32,256]{2,1,0:T(8,128)(2,1)}, bf16[8,32,512]{2,1,0:T(8,128)(2,1)}) custom-call(s32[8]{0:T(128)S(1)} %copy-done.2, bf16[128,16,128]{2,1,0:T(8,128)(2,1)S(1)} %all-to-all-done.1.ret_ref, s32[1,4096]{1,0:T(1,128)S(1)} %copy-done.3, bf16[8,32,256]{2,1,0:T(8,128)(2,1)S(1)} %copy-done.1, f32[8,32,512]{2,1,0:T(8,128)} %local.1.local_hbm, ...), custom_call_target="tpu_custom_call" | custom-call | flops 3000000000 | bytes 6000000 | tf_op jit(solution)/shard_map/back/pallas_call | solution.py:389
  (1 shorter events, 0.0 us)
Async XLA Ops:
  0.6 19.4 %copy-start = (bf16[64,128,128]{2,1,0:T(8,128)(2,1)S(1)}, bf16[64,128,128]{2,1,0:T(8,128)(2,1)}, u32[]{:S(2)}) copy-start(bf16[64,128,128]{2,1,0:T(8,128)(2,1)} %param.14) | copy-start | bytes 6291460
  8.5 25.8 %all-to-all-start = ((bf16[1152,2,128]{2,1,0:T(2,128)(2,1)}), bf16[1152,2,128]{2,1,0:T(2,128)(2,1)S(1)}, u32[]{:S(2)}, u32[]{:S(2)}) async-start(bf16[1152,2,128]{2,1,0:T(2,128)(2,1)} %bitcast.5), calls=%async_computation | async-start | bytes 1179648 | tf_op jit(solution)/shard_map/all_to_all | solution.py:352
  38.1 18.2 %all-to-all-start.1 = ((bf16[128,16,128]{2,1,0:T(8,128)(2,1)}), bf16[128,16,128]{2,1,0:T(8,128)(2,1)S(1)}, u32[]{:S(2)}, u32[]{:S(2)}) async-start(bf16[128,16,128]{2,1,0:T(8,128)(2,1)} %middle.1), calls=%async_computation.1 | async-start | bytes 1048576 | tf_op jit(solution)/shard_map/all_to_all | solution.py:387
  42.7 13.6 %copy-start.1 = (bf16[8,32,256]{2,1,0:T(8,128)(2,1)S(1)}, bf16[8,32,256]{2,1,0:T(8,128)(2,1)}, u32[]{:S(2)}) copy-start(bf16[8,32,256]{2,1,0:T(8,128)(2,1)} %ires_ref.1) | copy-start | bytes 393220
  42.7 13.6 %copy-start.2 = (s32[8]{0:T(128)S(1)}, s32[8]{0:T(128)}, u32[]{:S(2)}) copy-start(s32[8]{0:T(128)} %live_ref.3) | copy-start | bytes 100
  42.7 13.6 %copy-start.3 = (s32[1,4096]{1,0:T(1,128)S(1)}, s32[1,4096]{1,0:T(1,128)}, u32[]{:S(2)}) copy-start(s32[1,4096]{1,0:T(1,128)} %get-tuple-element.6.dest_ref) | copy-start | bytes 49156

commit v6 on v5

--- a/solution.py
+++ b/solution.py
@@ -241,9 +241,9 @@
         pltpu.make_async_copy(inv_hbm, inv_ref, sem.at[2]),
     ]
     stores = [
-        pltpu.make_async_copy(face_ref, face_hbm, out_sem.at[0]),
-        pltpu.make_async_copy(inner_ref, inner_hbm, out_sem.at[1]),
+        pltpu.make_async_copy(inner_ref.at[s], inner_hbm.at[s], out_sem.at[s]) for s in range(subs)
     ]
+    stores.append(pltpu.make_async_copy(face_ref, face_hbm, out_sem.at[subs]))
     for copy in loads:
         copy.start()
     senders = ret_ref.shape[0]
@@ -273,7 +273,7 @@
             correction = jnp.where(group_all == a, found[a * vecs:(a + 1) * vecs], correction)
         alive = lax.broadcasted_iota(jnp.int32, (vecs, face), 1) < live_ref[s]
         face_ref[s] = jnp.where(alive, local_ref[s] + correction, 0.0).astype(BF16)
-    stores[0].start()
+    stores[subs].start()
     for copy in loads[1:]:
         copy.wait()
     extended = [
@@ -281,7 +281,7 @@
     ]
     for s in range(subs):
         inner_ref[s] = dot_nt(extended[s], inv_ref[s]).astype(BF16)
-    stores[1].start()
+        stores[s].start()
     for copy in stores:
         copy.wait()
 
@@ -402,7 +402,7 @@
             VMEM((subs, vecs, inner), BF16),
             VMEM((subs, vecs, face), BF16),
             pltpu.SemaphoreType.DMA((3,)),
-            pltpu.SemaphoreType.DMA((2,)),
+            pltpu.SemaphoreType.DMA((subs + 1,)),
         ],
         cost_estimate=pl.CostEstimate(flops=3 * 10**9, bytes_accessed=6 * 10**6, transcendentals=0),
     )(live_count, returned, dest, interior_res, local, interior_inv, coupling)

time: 62 us -> 62.1 us (level)
  no operation moved by 1% of the time
where the time goes in v6:
time: 62.1 us; the launch traced here: 61.7 us
  waiting for transfers between devices  22.8 us (37%)
  Pallas kernels  22.1 us (36%)
  starting transfers between devices  16.1 us (26%)
  between operations  0.73 us (1%)
    all_to_all x1, waiting for transfers between devices, on_device(): lax.all_to_all(paired, AXES, split_axis=0, concat_axis=0, tiled=True)  14.3 us
    all_to_all x1, starting transfers between devices, on_device(): lax.all_to_all(paired, AXES, split_axis=0, concat_axis=0, tiled=True)  11.5 us
    all_to_all x1, waiting for transfers between devices, on_device(): lax.all_to_all(replies, AXES, split_axis=0, concat_axis=0, tiled=True)  8.52 us
    pallas_call x1, Pallas kernels, on_device(): pl.pallas_call(front_kernel, name='front', out_shape=(shape((subs, vecs,...  7.86 us
    pallas_call x1, Pallas kernels, on_device(): pl.pallas_call(back_kernel, name='back', compiler_params=pltpu.CompilerPa...  5.44 us
    pallas_call x1, Pallas kernels, on_device(): pl.pallas_call(local_kernel, name='local', compiler_params=pltpu.Compiler...  5.04 us
    all_to_all x1, starting transfers between devices, on_device(): lax.all_to_all(replies, AXES, split_axis=0, concat_axis=0, tiled=True)  4.58 us
    pallas_call x1, Pallas kernels, on_device(): pl.pallas_call(middle_kernel, name='middle', compiler_params=pltpu.Compil...  3.75 us
  transfers between devices with their start and end apart: 2, of which 2 were waited for; matrix products, arithmetic and copies ran while one was open for 0% of the time, Pallas kernels for 8%

profile of v6, /device:TPU:1, one launch (start us, length us, event | category | flops | bytes accessed | tf_op | source)
XLA Modules:
  0.0 61.7 jit_solution(5304771237250650550)
XLA Ops:
  0.6 0.0 copy-start
  0.6 7.9 %front.1 = (bf16[8,32,512]{2,1,0:T(8,128)(2,1)}, bf16[2304,128]{1,0:T(8,128)(2,1)}, s32[1,4096]{1,0:T(1,128)}) custom-call(s32[8]{0:T(128)} %live_ref.3, s32[1,4096]{1,0:T(1,128)} %bitcast.6, s32[1,4096]{1,0:T(1,128)} %bitcast.7, bf16[8,32,256]{2,1,0:T(8,128)(2,1)} %ires_ref.1, bf16[8,32,512]{2,1,0:T(8,128)(2,1)} %fres_hbm.1, bf16[8,256,256]{2,1,0:T(8,128)(2,1)} %inv_hbm.3, ...), custom_call_target="tpu_custom_call" | custom-call | flops 3000000000 | bytes 5000000 | tf_op jit(solution)/shard_map/front/pallas_call | solution.py:316
  8.5 11.5 %all-to-all-start = ((bf16[1152,2,128]{2,1,0:T(2,128)(2,1)}), bf16[1152,2,128]{2,1,0:T(2,128)(2,1)S(1)}, u32[]{:S(2)}, u32[]{:S(2)}) async-start(bf16[1152,2,128]{2,1,0:T(2,128)(2,1)} %bitcast.5), calls=%async_computation | async-start | bytes 1179648 | tf_op jit(solution)/shard_map/all_to_all | solution.py:352
  20.0 0.0 copy-done
  20.1 14.3 %all-to-all-done = bf16[1152,2,128]{2,1,0:T(2,128)(2,1)S(1)} async-done(((bf16[1152,2,128]{2,1,0:T(2,128)(2,1)}), bf16[1152,2,128]{2,1,0:T(2,128)(2,1)S(1)}, u32[]{:S(2)}, u32[]{:S(2)}) %all-to-all-start) | async-done | bytes 589856 | tf_op jit(solution)/shard_map/all_to_all | solution.py:352
  34.3 3.7 %middle.1 = bf16[128,16,128]{2,1,0:T(8,128)(2,1)} custom-call(bf16[2304,128]{1,0:T(8,128)(2,1)S(1)} %bitcast.4, bf16[4,128,128]{2,1,0:T(8,128)(2,1)S(1)} %constant_dynamic-slice_fusion.inv_ref), custom_call_target="tpu_custom_call" | custom-call | flops 1000000000 | bytes 2000000 | tf_op jit(solution)/shard_map/middle/pallas_call | solution.py:370
  38.1 4.6 %all-to-all-start.1 = ((bf16[128,16,128]{2,1,0:T(8,128)(2,1)}), bf16[128,16,128]{2,1,0:T(8,128)(2,1)S(1)}, u32[]{:S(2)}, u32[]{:S(2)}) async-start(bf16[128,16,128]{2,1,0:T(8,128)(2,1)} %middle.1), calls=%async_computation.1 | async-start | bytes 1048576 | tf_op jit(solution)/shard_map/all_to_all | solution.py:387
  42.7 0.0 copy-start.1
  42.7 0.0 copy-start.2
  42.7 0.0 copy-start.3
  42.7 5.0 %local.1.local_hbm = f32[8,32,512]{2,1,0:T(8,128)} custom-call(bf16[8,32,512]{2,1,0:T(8,128)(2,1)} %get-tuple-element.7.cond_ref, bf16[8,512,512]{2,1,0:T(8,128)(2,1)} %schur_hbm.1), custom_call_target="tpu_custom_call" | custom-call | flops 134217728 | bytes 5000000 | tf_op jit(solution)/shard_map/local/pallas_call | solution.py:355
  47.8 8.5 %all-to-all-done.1.ret_ref = bf16[128,16,128]{2,1,0:T(8,128)(2,1)S(1)} async-done(((bf16[128,16,128]{2,1,0:T(8,128)(2,1)}), bf16[128,16,128]{2,1,0:T(8,128)(2,1)S(1)}, u32[]{:S(2)}, u32[]{:S(2)}) %all-to-all-start.1) | async-done | bytes 524320 | tf_op jit(solution)/shard_map/all_to_all | solution.py:387
  56.3 0.0 copy-done.1
  56.3 0.0 copy-done.2
  56.3 0.0 copy-done.3
  56.3 5.4 %back.1 = (bf16[8,32,256]{2,1,0:T(8,128)(2,1)}, bf16[8,32,512]{2,1,0:T(8,128)(2,1)}) custom-call(s32[8]{0:T(128)S(1)} %copy-done.2, bf16[128,16,128]{2,1,0:T(8,128)(2,1)S(1)} %all-to-all-done.1.ret_ref, s32[1,4096]{1,0:T(1,128)S(1)} %copy-done.3, bf16[8,32,256]{2,1,0:T(8,128)(2,1)S(1)} %copy-done.1, f32[8,32,512]{2,1,0:T(8,128)} %local.1.local_hbm, ...), custom_call_target="tpu_custom_call" | custom-call | flops 3000000000 | bytes 6000000 | tf_op jit(solution)/shard_map/back/pallas_call | solution.py:389
  (1 shorter events, 0.0 us)
Async XLA Ops:
  0.6 19.4 %copy-start = (bf16[64,128,128]{2,1,0:T(8,128)(2,1)S(1)}, bf16[64,128,128]{2,1,0:T(8,128)(2,1)}, u32[]{:S(2)}) copy-start(bf16[64,128,128]{2,1,0:T(8,128)(2,1)} %param.14) | copy-start | bytes 6291460
  8.5 25.8 %all-to-all-start = ((bf16[1152,2,128]{2,1,0:T(2,128)(2,1)}), bf16[1152,2,128]{2,1,0:T(2,128)(2,1)S(1)}, u32[]{:S(2)}, u32[]{:S(2)}) async-start(bf16[1152,2,128]{2,1,0:T(2,128)(2,1)} %bitcast.5), calls=%async_computation | async-start | bytes 1179648 | tf_op jit(solution)/shard_map/all_to_all | solution.py:352
  38.1 18.2 %all-to-all-start.1 = ((bf16[128,16,128]{2,1,0:T(8,128)(2,1)}), bf16[128,16,128]{2,1,0:T(8,128)(2,1)S(1)}, u32[]{:S(2)}, u32[]{:S(2)}) async-start(bf16[128,16,128]{2,1,0:T(8,128)(2,1)} %middle.1), calls=%async_computation.1 | async-start | bytes 1048576 | tf_op jit(solution)/shard_map/all_to_all | solution.py:387
  42.7 13.6 %copy-start.1 = (bf16[8,32,256]{2,1,0:T(8,128)(2,1)S(1)}, bf16[8,32,256]{2,1,0:T(8,128)(2,1)}, u32[]{:S(2)}) copy-start(bf16[8,32,256]{2,1,0:T(8,128)(2,1)} %ires_ref.1) | copy-start | bytes 393220
  42.7 13.6 %copy-start.2 = (s32[8]{0:T(128)S(1)}, s32[8]{0:T(128)}, u32[]{:S(2)}) copy-start(s32[8]{0:T(128)} %live_ref.3) | copy-start | bytes 100
  42.7 13.6 %copy-start.3 = (s32[1,4096]{1,0:T(1,128)S(1)}, s32[1,4096]{1,0:T(1,128)}, u32[]{:S(2)}) copy-start(s32[1,4096]{1,0:T(1,128)} %get-tuple-element.6.dest_ref) | copy-start | bytes 49156
